TPU v7x, 128 devices: a whole 4x4x4 slice. The times are simulated.
128 devices in a mesh: dp: 16 (over y, x_hi, core), rows: 8 (over z, x_lo).
Axes of the slice: x: 4 (x_hi: 2, x_lo: 2; x = x_hi * 2 + x_lo), y: 4, z: 4, core: 2. Of those that a mesh axis runs over, the one named last changes fastest.
Arguments:
- images: bfloat16 [16, 24, 48, 1280], P('dp', 'rows'), may hold values from -6 to 6
- cotangent: bfloat16 [16, 24, 48, 1280], P('dp', 'rows'), may hold values from -6 to 6
- first_weight: bfloat16 [16, 8, 9, 12800], P('dp', 'rows'), may hold values from -0.0546875 to 0.0546875
- second_weight: bfloat16 [16, 8, 9, 12800], P('dp', 'rows'), may hold values from -0.0546875 to 0.0546875
- first_basis: float32 [64, 1280], replicated, may hold values from -0.15625 to 0.15625
- second_basis: float32 [64, 1280], replicated, may hold values from -0.15625 to 0.15625
Outputs:
- block_output: bfloat16 [16, 24, 48, 1280], P('dp', 'rows')
- first_grad: float32 [16, 8, 9, 12800], P('dp', 'rows')
- second_grad: float32 [16, 8, 9, 12800], P('dp', 'rows')
All inputs are finite; a program needn't handle non-finite values.
Results may differ from a plain program's by a relative error of at most 0.014.
Values may be sent and summed in bfloat16 or wider, within the bound.
A program may use at most 192 MiB of HBM per device.

v0:
```python
import math

import jax
import jax.numpy as jnp
from jax import lax
from jax.sharding import PartitionSpec as P

CHANNELS = 1280
GROUPS = 32
LAT_W = 48
BAND = 3
IMG_DEV = 1


def normalize(values):
    full_shape = values.shape
    size_group = CHANNELS // GROUPS
    grouped = values.reshape(full_shape[:-1] + (full_shape[-1] // size_group, size_group))
    center = jnp.mean(grouped, axis=(1, 2, 4), keepdims=True)
    spread = jnp.mean(jnp.square(grouped - center), axis=(1, 2, 4), keepdims=True)
    return ((grouped - center) / jnp.sqrt(spread + 1e-05)).reshape(full_shape)


def activate(values):
    return jax.nn.silu(normalize(values))


def convolve(inputs, kernel, form):
    padded = jnp.pad(inputs, ((0, 0), (1, 1), (1, 1), (0, 0)))
    height = inputs.shape[1]
    width = inputs.shape[2]
    summed = None
    for row_tap in range(3):
        for col_tap in range(3):
            window = padded[:, row_tap : row_tap + height, col_tap : col_tap + width]
            term = jnp.einsum(
                form, window, kernel[row_tap, col_tap], preferred_element_type=jnp.float32
            )
            summed = term if summed is None else summed + term
    return summed


def weight_grad(inputs, grads, form):
    padded = jnp.pad(inputs, ((0, 0), (1, 1), (1, 1), (0, 0)))
    height = inputs.shape[1]
    width = inputs.shape[2]
    taps = []
    for row_tap in range(3):
        row_list = []
        for col_tap in range(3):
            window = padded[:, row_tap : row_tap + height, col_tap : col_tap + width]
            row_list.append(jnp.einsum(form, window, grads, preferred_element_type=jnp.float32))
        taps.append(jnp.stack(row_list))
    return jnp.stack(taps)


def coefficients(raw_grad, basis):
    return jnp.einsum("abcd,rc->abrd", raw_grad, basis, precision=lax.Precision.HIGHEST)


def expand(basis, coefficient):
    return jnp.einsum("rc,abrd->abcd", basis, coefficient, precision=lax.Precision.HIGHEST)


def body(images, cotangent, first_weight, second_weight, first_basis, second_basis):
    dp_width = CHANNELS // lax.axis_size("dp")
    rows_width = CHANNELS // lax.axis_size("rows")
    grad_scale = 1.0 / math.sqrt(
        lax.axis_size("dp") * IMG_DEV * BAND * lax.axis_size("rows") * LAT_W
    )
    whole_images, whole_cotangent = (
        lax.all_gather(images, "rows", axis=1, tiled=True),
        lax.all_gather(cotangent, "rows", axis=1, tiled=True),
    )
    first_flat = lax.all_gather(first_weight, "dp", axis=3, tiled=True)
    first_full = first_flat.reshape(3, 3, CHANNELS, rows_width)
    activated = activate(whole_images.astype(jnp.float32)).astype(jnp.bfloat16)
    first_out = convolve(activated, first_full, "nhwc,cd->nhwd")
    hidden = activate(first_out).astype(jnp.bfloat16)
    second_flat = lax.all_gather(second_weight, "dp", axis=3, tiled=True)
    second_full = second_flat.reshape(3, 3, CHANNELS, rows_width)
    partial_sums = convolve(hidden, second_full, "nhwc,dc->nhwd")
    band_sums = lax.psum_scatter(
        partial_sums.astype(jnp.bfloat16), "rows", scatter_dimension=1, tiled=True
    ).astype(jnp.float32)
    block_output = (images.astype(jnp.float32) + band_sums).astype(jnp.bfloat16)
    hidden_grad = convolve(whole_cotangent, second_full[::-1, ::-1], "nhwc,cd->nhwd")
    unused, pullback = jax.vjp(activate, first_out)
    pre_grad = pullback(hidden_grad)[0].astype(jnp.bfloat16)
    second_terms = weight_grad(hidden, whole_cotangent, "nhwc,nhwd->dc")
    second_shard = lax.psum_scatter(
        second_terms.astype(jnp.bfloat16), "dp", scatter_dimension=2, tiled=True
    ).astype(jnp.float32)
    basis_rows = lax.dynamic_slice_in_dim(
        second_basis, lax.axis_index("rows") * rows_width, rows_width, 1
    )
    second_coeff = jnp.einsum(
        "abdc,rc->abdr", second_shard, basis_rows, precision=lax.Precision.HIGHEST
    )
    second_sums = lax.psum(second_coeff.astype(jnp.bfloat16), "rows").astype(jnp.float32)
    second_back = jnp.einsum(
        "rc,abdr->abdc", basis_rows, second_sums, precision=lax.Precision.HIGHEST
    )
    second_grad = ((second_shard - second_back) * grad_scale).reshape(
        1, 1, 9, dp_width * rows_width
    )
    basis_images = lax.dynamic_slice_in_dim(
        first_basis, lax.axis_index("dp") * dp_width, dp_width, 1
    )
    first_shard = lax.psum_scatter(
        weight_grad(activated, pre_grad, "nhwc,nhwd->cd").astype(jnp.bfloat16),
        "dp",
        scatter_dimension=2,
        tiled=True,
    ).astype(jnp.float32)
    first_sums = lax.psum(
        coefficients(first_shard, basis_images).astype(jnp.bfloat16), "dp"
    ).astype(jnp.float32)
    first_grad = (first_shard - expand(basis_images, first_sums)) * grad_scale
    first_grad = first_grad.reshape(1, 1, 9, dp_width * rows_width)
    return (block_output, first_grad, second_grad)


def solution(mesh):
    return jax.shard_map(
        body,
        mesh=mesh,
        in_specs=(
            P("dp", "rows", None, None),
            P("dp", "rows", None, None),
            P("dp", "rows", None, None),
            P("dp", "rows", None, None),
            P(),
            P(),
        ),
        out_specs=(
            P("dp", "rows", None, None),
            P("dp", "rows", None, None),
            P("dp", "rows", None, None),
        ),
        check_vma=False,
    )
```

profile of v0, /device:TPU:0, one launch (start us, length us, event | category | flops | bytes accessed | tf_op | source)
XLA Modules:
  0.0 784.4 jit_solution(11428268481880192215)
XLA Ops:
  10.0 70.2 %all-gather.5.cloned.1.call-done = bf16[1,24,48,1280]{3,2,0,1:T(8,128)(2,1)} async-done(((bf16[1,3,48,1280]{3,2,0,1:T(8,128)(2,1)}), bf16[1,24,48,1280]{3,2,0,1:T(8,128)(2,1)}) %all-gather.5.cloned.1.call-update) | async-done | bytes 2949136 | tf_op jit(solution)/shard_map/all_gather | solution.py:72
  80.2 2.5 convert_reduce_fusion
  84.3 3.0 multiply_convert_fusion
  87.3 59.4 %all-gather.7.cloned.1.call-done = bf16[1,1,9,204800]{3,2,1,0:T(8,128)(2,1)} async-done(((bf16[1,1,9,12800]{3,2,1,0:T(8,128)(2,1)}), bf16[1,1,9,204800]{3,2,1,0:T(8,128)(2,1)}) %all-gather.7.cloned.1.call-update) | async-done | bytes 3686416 | tf_op jit(solution)/shard_map/all_gather | solution.py:75
  146.8 15.0 %reshape.402 = bf16[3,3,1280,160]{3,2,1,0:T(8,128)(2,1)} reshape(bf16[1,1,9,204800]{3,2,1,0:T(8,128)(2,1)} %all-gather.7.cloned.1.call-done) | data formatting | bytes 7372800 | tf_op jit(solution)/shard_map/reshape | solution.py:76
  161.8 2.2 fusion.185
  175.9 35.9 %all-gather.9.cloned.1.call-done = bf16[1,1,9,204800]{3,2,1,0:T(8,128)(2,1)} async-done(((bf16[1,1,9,12800]{3,2,1,0:T(8,128)(2,1)}), bf16[1,1,9,204800]{3,2,1,0:T(8,128)(2,1)}) %all-gather.9.cloned.1.call-update) | async-done | bytes 3686416 | tf_op jit(solution)/shard_map/all_gather | solution.py:80
  211.9 15.4 %reshape.412 = bf16[3,3,1280,160]{3,2,1,0:T(8,128)(2,1)} reshape(bf16[1,1,9,204800]{3,2,1,0:T(8,128)(2,1)} %all-gather.9.cloned.1.call-done) | data formatting | bytes 7372800 | tf_op jit(solution)/shard_map/reshape | solution.py:81
  227.2 52.1 %all-gather.11.cloned.1.call-done = bf16[1,24,48,1280]{3,2,0,1:T(8,128)(2,1)} async-done(((bf16[1,3,48,1280]{3,2,0,1:T(8,128)(2,1)}), bf16[1,24,48,1280]{3,2,0,1:T(8,128)(2,1)}) %all-gather.11.cloned.1.call-update) | async-done | bytes 2949136 | tf_op jit(solution)/shard_map/all_gather | solution.py:73
  279.3 3.0 fusion.13
  283.0 2.9 fusion.235
  295.2 3.0 fusion.158
  308.5 12.1 %copy.96 = bf16[3,3,1280,160]{3,1,0,2:T(4,128)(2,1)} copy(bf16[3,3,1280,160]{2,3,1,0:T(8,128)(2,1)} %pad_maximum_fusion) | data formatting | bytes 7372800
  320.6 14.4 %reshape.471 = bf16[1280,1440]{1,0:T(8,128)(2,1)} reshape(bf16[1280,3,3,160]{3,2,1,0:T(4,128)(2,1)} %bitcast.589) | data formatting | bytes 7372800
  335.3 2.7 fusion.149
  344.4 2.1 pad_maximum_fusion.1
  346.5 12.3 %copy.98 = bf16[3,3,1280,160]{3,1,0,2:T(4,128)(2,1)} copy(bf16[3,3,1280,160]{2,3,1,0:T(8,128)(2,1)} %pad_maximum_fusion.1) | data formatting | bytes 7372800
  358.8 14.5 %reshape.473 = bf16[1280,1440]{1,0:T(8,128)(2,1)} reshape(bf16[1280,3,3,160]{3,2,1,0:T(4,128)(2,1)} %bitcast.590) | data formatting | bytes 7372800
  373.9 4.8 fusion.255
  378.7 4.7 fusion.256
  383.3 4.6 fusion.257
  388.0 3.5 fusion.259
  391.5 3.5 fusion.260
  394.9 3.5 fusion.261
  398.4 3.6 fusion.254
  402.0 3.6 fusion.258
  405.6 7.7 reduce-scatter.10.cloned.1.call-done
  415.3 79.6 %reduce-scatter.12.cloned.1.call-done = bf16[80,1440]{1,0:T(8,128)(2,1)} async-done(((bf16[1280,1440]{1,0:T(8,128)(2,1)}), bf16[80,1440]{1,0:T(8,128)(2,1)}) %reduce-scatter.12.cloned.1.call-update) | async-done | bytes 230416
  500.8 17.8 %fusion.3 = bf16[1,24,48,1280]{3,2,1,0:T(8,128)(2,1)} fusion(f32[24,48,1280]{2,1,0:T(8,128)} %fusion.261, f32[24,48,1280]{2,1,0:T(8,128)} %fusion.260, f32[24,48,1280]{2,1,0:T(8,128)} %fusion.259, f32[24,48,1280]{2,1,0:T(8,128)} %fusion.258, f32[24,48,1280]{2,1,0:T(8,128)} %fusion.257, f32[24,48,1280]{2,1,0:T(8,128)} %fusion.256, ...), kind=kOutput, calls=%fused_computation.9 | convolution fusion | flops 485130240 | bytes 51159040 | tf_op jit(solution)/shard_map/nhwc,dc->nhwd/dot_general | solution.py:36
  518.5 51.8 %all-reduce.8.cloned.1.call-done = bf16[3,3,80,64]{2,3,1,0:T(8,128)(2,1)} async-done(((bf16[3,3,80,64]{2,3,1,0:T(8,128)(2,1)}), bf16[3,3,80,64]{2,3,1,0:T(8,128)(2,1)}) %all-reduce.8.cloned.1.call-update) | async-done | bytes 92176 | tf_op jit(solution)/shard_map/psum | solution.py:100
  573.9 132.7 %all-reduce.6.cloned.1.call-done = bf16[3,3,64,160]{3,2,1,0:T(8,128)(2,1)} async-done(((bf16[3,3,64,160]{3,2,1,0:T(8,128)(2,1)}), bf16[3,3,64,160]{3,2,1,0:T(8,128)(2,1)}) %all-reduce.6.cloned.1.call-update) | async-done | bytes 184336 | tf_op jit(solution)/shard_map/psum | solution.py:116
  710.2 65.6 %reduce-scatter.8.cloned.1.call-done = bf16[1,3,48,1280]{3,2,1,0:T(8,128)(2,1)} async-done(((bf16[1,24,48,1280]{3,2,1,0:T(8,128)(2,1)}), bf16[1,3,48,1280]{3,2,1,0:T(8,128)(2,1)}) %reduce-scatter.8.cloned.1.call-update) | async-done | bytes 368656 | tf_op jit(solution)/shard_map/reduce_scatter | solution.py:83
  (130 shorter events, 60.3 us)
Async XLA Ops:
  7.2 491.8 %copy-start = (f32[64,1280]{1,0:T(8,128)S(1)}, f32[64,1280]{1,0:T(8,128)}, u32[]{:S(2)}) copy-start(f32[64,1280]{1,0:T(8,128)} %param.10) | copy-start | bytes 983044
  7.2 73.0 %all-gather.5.cloned.1.call-start = ((), (), s32[]{:S(2)}) async-start(), calls=%async_computation.3 | async-start | bytes 3317760 | tf_op jit(solution)/shard_map/all_gather | solution.py:72
  7.9 138.8 %all-gather.7.cloned.1.call-start = ((), (), s32[]{:S(2)}) async-start(), calls=%async_computation.4 | async-start | bytes 6963200 | tf_op jit(solution)/shard_map/all_gather | solution.py:75
  8.7 203.2 %all-gather.9.cloned.1.call-start = ((), (), s32[]{:S(2)}) async-start(), calls=%async_computation.5 | async-start | bytes 6963200 | tf_op jit(solution)/shard_map/all_gather | solution.py:80
  9.4 269.9 %all-gather.11.cloned.1.call-start = ((), (), s32[]{:S(2)}) async-start(), calls=%async_computation.7 | async-start | bytes 3317760 | tf_op jit(solution)/shard_map/all_gather | solution.py:73
  10.0 403.3 %reduce-scatter.10.cloned.1.call-start = ((), (), s32[]{:S(2)}) async-start(), calls=%async_computation.10 | async-start | bytes 4177920
  80.2 2.8 copy-start.1
  87.3 74.5 %copy-start.3 = (bf16[1,24,48,1280]{3,2,1,0:T(8,128)(2,1)S(1)}, bf16[1,24,48,1280]{3,2,1,0:T(8,128)(2,1)}, u32[]{:S(2)}) copy-start(bf16[1,24,48,1280]{3,2,1,0:T(8,128)(2,1)} %multiply_convert_fusion) | copy-start | bytes 8847364
  161.8 2.9 copy-start.6
  279.3 3.7 copy-start.2
  283.0 2.9 copy-start.7
  290.7 1.3 copy-start.5
  295.2 3.0 copy-start.4
  335.0 159.9 %reduce-scatter.12.cloned.1.call-start = ((), (), s32[]{:S(2)}) async-start(), calls=%async_computation.11 | async-start | bytes 4177920
  335.3 2.7 copy-start.8
  373.3 197.0 %all-reduce.8.cloned.1.call-start = ((), (), s32[]{:S(2)}) async-start(), calls=%async_computation.9 | async-start | bytes 294912 | tf_op jit(solution)/shard_map/psum | solution.py:100
  373.9 14.1 %slice-start = ((s8[5898240]{0:T(1024)(128)(4,1)}), s8[4194304]{0:T(1024)(128)(4,1)S(1)}, s32[]{:S(2)}) async-start(s8[5898240]{0:T(1024)(128)(4,1)} %bitcast.591), calls=%async_computation.12 | async-start | bytes 8388608
  378.7 9.3 %slice-start.1 = ((s8[5898240]{0:T(1024)(128)(4,1)}), s8[1703936]{0:T(1024)(128)(4,1)S(1)}, s32[]{:S(2)}) async-start(s8[5898240]{0:T(1024)(128)(4,1)} %bitcast.591), calls=%async_computation.13 | async-start | bytes 3407872
  498.9 207.8 %all-reduce.6.cloned.1.call-start = ((), (), s32[]{:S(2)}) async-start(), calls=%async_computation.8 | async-start | bytes 589824 | tf_op jit(solution)/shard_map/psum | solution.py:116
  500.5 275.3 %reduce-scatter.8.cloned.1.call-start = ((), (), s32[]{:S(2)}) async-start(), calls=%async_computation.6 | async-start | bytes 3317760 | tf_op jit(solution)/shard_map/reduce_scatter | solution.py:83
  572.3 203.6 %copy-start.9 = (bf16[1,3,48,1280]{3,2,1,0:T(8,128)(2,1)S(1)}, bf16[1,3,48,1280]{3,2,1,0:T(8,128)(2,1)}, u32[]{:S(2)}) copy-start(bf16[1,3,48,1280]{3,2,1,0:T(8,128)(2,1)} %param.6) | copy-start | bytes 1105924
Sparse Core Ops, SparseCore 0:
  9.6 70.5 all-gather.4
  82.7 64.0 all-gather.6
  149.2 62.5 all-gather.8
  213.4 65.8 all-gather.10
  335.1 78.0 reduce-scatter.9
  417.2 77.5 reduce-scatter.11
  499.0 71.3 all-reduce.7
  573.4 133.1 all-reduce.5
  709.1 66.7 reduce-scatter.7
where the time goes:
time: 794 us; the launch traced here: 784 us
  waiting for transfers between devices  558 us (70%)
  matrix products  99.6 us (13%)
  local copies, waits for them, and re-layouts  95.2 us (12%)
  other arithmetic  16.1 us (2%)
  between operations  14.5 us (2%)
    psum x1, waiting for transfers between devices, body(): lax.psum(coefficients(first_shard, basis_images).astype(jnp.bfloat16), 'dp')  133 us
    unnamed x11, waiting for transfers between devices  89.9 us
    dot_general x27, matrix products, convolve(): jnp.einsum(form, window, kernel[row_tap, col_tap], preferred_element_type...  73.6 us
    all_gather x1, waiting for transfers between devices, body(): lax.all_gather(images, 'rows', axis=1, tiled=True)  70.2 us
    reduce_scatter x1, waiting for transfers between devices, body(): lax.psum_scatter(partial_sums.astype(jnp.bfloat16), 'rows', scatter_dimen...  65.6 us
    all_gather x1, waiting for transfers between devices, body(): first_flat = lax.all_gather(first_weight, 'dp', axis=3, tiled=True)  59.4 us
    unnamed x32, local copies, waits for them, and re-layouts  59.1 us
    all_gather x1, waiting for transfers between devices, body(): lax.all_gather(cotangent, 'rows', axis=1, tiled=True)  52.1 us
  transfers between devices with their start and end apart: 9, of which 9 were waited for; matrix products, arithmetic and copies ran while one was open for 19% of the time, Pallas kernels for 0%

commit v1 on v0

v1 whole, which is shorter than its diff:
```python
import math

import jax
import jax.numpy as jnp
from jax import lax
from jax.experimental import pallas as pl
from jax.experimental.pallas import tpu as pltpu
from jax.sharding import PartitionSpec as P

C = 1280
GSIZE = 40
W = 48
H = 24
PIX = W * H
BAND = 144
DPW = 80
RW = 160
Q = 512
K3 = 3 * Q
RANK = 64
EPS = 1e-05
F32 = jnp.float32
BF16 = jnp.bfloat16
MESH = pl.DeviceIdType.MESH
HIGH = lax.Precision.HIGHEST
N_SEM = 104


def dot(a, b):
    return jnp.dot(a, b, preferred_element_type=F32)


def dot_nt(a, b):
    return lax.dot_general(a, b, (((1,), (1,)), ((), ())), preferred_element_type=F32)


def group_matrix(rows, channel_of):
    channel = channel_of(lax.broadcasted_iota(jnp.int32, (rows, 128), 0))
    group = lax.broadcasted_iota(jnp.int32, (rows, 128), 1) * GSIZE
    return jnp.where((channel >= group) & (channel < group + GSIZE), 1.0, 0.0).astype(F32)


def group_mean(sums, groups):
    per_group = jnp.sum(jnp.dot(sums, groups, precision=HIGH, preferred_element_type=F32), axis=0, keepdims=True)
    spread = lax.dot_general(
        jnp.broadcast_to(per_group, (8, 128)), groups, (((1,), (1,)), ((), ())),
        precision=HIGH, preferred_element_type=F32,
    )
    return spread[0:1] * (1.0 / (PIX * GSIZE))


def fold8(values):
    total = values[0:8]
    for at in range(8, values.shape[0], 8):
        total = total + values[at : at + 8]
    return total


def split(values):
    high = values.astype(BF16)
    low = (values - high.astype(F32)).astype(BF16)
    return high, low


def kernel(
    img, cot, w1r, w2r, b1, b2, out, g1, g2,
    imgf, cotp, w1, w2, actp, x, s, du, hidc, hp, pp, act_t, cot_t,
    o, qa, qb, qd, qv, hb, hx, hpair, gr, gc, gt, ga, gb, gd, gu, bs1, bs2,
    ssem, rsem,
):
    dp = lax.axis_index("dp")
    rows = lax.axis_index("rows")
    core = lax.rem(dp, 2)
    xh = lax.rem(dp // 2, 2)
    y = dp // 4
    xl = lax.rem(rows, 2)
    z = rows // 2
    zp, zm, z2 = lax.rem(z + 1, 4), lax.rem(z + 3, 4), lax.rem(z + 2, 4)
    yp, ym, y2 = lax.rem(y + 1, 4), lax.rem(y + 3, 4), lax.rem(y + 2, 4)
    ZP, ZM = (dp, zp * 2 + xl), (dp, zm * 2 + xl)
    XN = (dp, z * 2 + 1 - xl)
    YP, YM = (yp * 4 + xh * 2 + core, rows), (ym * 4 + xh * 2 + core, rows)
    XH = (y * 4 + (1 - xh) * 2 + core, rows)
    CN = (y * 4 + xh * 2 + 1 - core, rows)
    pending = []

    def send(src, dst, device):
        at = len(pending)
        copy = pltpu.make_async_remote_copy(
            src_ref=src, dst_ref=dst, send_sem=ssem.at[at], recv_sem=rsem.at[at],
            device_id=device, device_id_type=MESH,
        )
        copy.start()
        pending.append(copy)
        return copy

    def gather_rows(src, full, base):
        def at(zz, xx, low=0, size=BAND):
            return full.at[pl.ds(pl.multiple_of(base + (zz * 2 + xx) * BAND + low, 16), size)]

        def pass_on(piece, device):
            return send(piece, piece, device)

        own = at(z, xl)
        cx, cp, cm = send(src, own, XN), send(src, own, ZP), send(src, own, ZM)
        yield
        cx.wait_recv()
        ep, em = pass_on(at(z, 1 - xl), ZP), pass_on(at(z, 1 - xl), ZM)
        yield
        cp.wait_recv()
        fp = pass_on(at(zm, xl, 0, 80), ZP)
        cm.wait_recv()
        fm = pass_on(at(zp, xl, 80, 64), ZM)
        yield
        ep.wait_recv()
        hp_ = pass_on(at(zm, 1 - xl, 0, 80), ZP)
        em.wait_recv()
        hm_ = pass_on(at(zp, 1 - xl, 80, 64), ZM)
        yield
        for copy in (fp, fm, hp_, hm_):
            copy.wait_recv()
        yield

    def gather_weight(full):
        def at(yy, hh, low=0, size=DPW):
            return full.at[pl.ds(pl.multiple_of(((yy * 2 + hh) * 2 + core) * DPW + low, 16), size)]

        def pass_on(piece, device):
            return send(piece, piece, device)

        own = at(y, xh)
        ax, ap, am, ac = (pass_on(own, device) for device in (XH, YP, YM, CN))
        yield
        ax.wait_recv()
        bp, bm, bc = (pass_on(at(y, 1 - xh), device) for device in (YP, YM, CN))
        yield
        ap.wait_recv()
        fp, fc = pass_on(at(ym, xh, 0, 48), YP), pass_on(at(ym, xh), CN)
        am.wait_recv()
        fm, fd = pass_on(at(yp, xh, 48, 32), YM), pass_on(at(yp, xh), CN)
        yield
        bp.wait_recv()
        hp_, hc = pass_on(at(ym, 1 - xh, 0, 48), YP), pass_on(at(ym, 1 - xh), CN)
        bm.wait_recv()
        hm_, hd = pass_on(at(yp, 1 - xh, 48, 32), YM), pass_on(at(yp, 1 - xh), CN)
        yield
        last = []
        fp.wait_recv()
        last.append(pass_on(at(y2, xh, 0, 48), CN))
        fm.wait_recv()
        last.append(pass_on(at(y2, xh, 48, 32), CN))
        hp_.wait_recv()
        last.append(pass_on(at(y2, 1 - xh, 0, 48), CN))
        hm_.wait_recv()
        last.append(pass_on(at(y2, 1 - xh, 48, 32), CN))
        yield
        for copy in [ac, bc, fc, fd, hc, hd] + last:
            copy.wait_recv()
        yield

    scale = 1.0 / math.sqrt(16 * PIX)

    def scatter_grad(n, grad_out, p):
        c = send(gr.at[n, :, 1 - core], gc.at[n], CN)
        yield
        c.wait_recv()
        for block in range(8):
            gt[n, block] = (gr[n, block, core].astype(F32) + gc[n, block].astype(F32)).astype(BF16)
        ap = send(gt.at[n, y2 * 2], ga.at[n, 0], YP)
        am = send(gt.at[n, y2 * 2 + 1], ga.at[n, 1], YM)
        yield
        ap.wait_recv()
        gt[n, yp * 2] = (gt[n, yp * 2].astype(F32) + ga[n, 0].astype(F32)).astype(BF16)
        bp = send(gt.at[n, pl.ds(yp * 2, 2)], gb.at[n, 0], YP)
        am.wait_recv()
        gt[n, ym * 2 + 1] = (gt[n, ym * 2 + 1].astype(F32) + ga[n, 1].astype(F32)).astype(BF16)
        bm = send(gt.at[n, pl.ds(ym * 2, 2)], gb.at[n, 1], YM)
        yield
        bp.wait_recv()
        bm.wait_recv()

        def mine(h):
            return gt[n, y * 2 + h].astype(F32) + gb[n, 0, h].astype(F32) + gb[n, 1, h].astype(F32)

        gu[n] = mine(1 - xh).astype(BF16)
        d = send(gu.at[n], gd.at[n], XH)
        yield
        d.wait_recv()
        total = (mine(xh) + gd[n].astype(F32)) * scale
        rest = total[:, 384:512]
        for q in range(3):
            grad_out[p * 3 + q, :, 0:128] = total[:, q * 128 : q * 128 + 128]
            turned = rest if q == 0 else pltpu.roll(rest, 128 - 32 * q, 1)
            grad_out[p * 3 + q, :, 128:160] = turned[:, 0:32]
        yield

    def step(*work):
        for one in work:
            next(one)

    for raw, full in ((w1r, w1), (w2r, w2)):
        mine_at = pl.ds(pl.multiple_of(dp * DPW, 16), DPW)
        for p in range(3):
            rest = jnp.zeros((DPW, 128), F32)
            lane = lax.broadcasted_iota(jnp.int32, (DPW, 128), 1)
            for q in range(3):
                full[mine_at, p * Q + q * 128 : p * Q + q * 128 + 128] = raw[p * 3 + q, :, 0:128]
                tail = jnp.concatenate(
                    [raw[p * 3 + q, :, 128:160].astype(F32), jnp.zeros((DPW, 96), F32)], axis=1
                )
                rest = rest + (tail if q == 0 else pltpu.roll(tail, 32 * q, 1))
            full[mine_at, p * Q + 384 : p * Q + 512] = rest.astype(BF16)

    barrier = pltpu.get_barrier_semaphore()
    for device in (ZP, ZM, XN, YP, YM, XH, CN):
        pl.semaphore_signal(barrier, inc=1, device_id=device, device_id_type=MESH)
    pl.semaphore_wait(barrier, 7)

    get_img = gather_rows(img, imgf, 0)
    get_w1 = gather_weight(w1)
    get_cot = gather_rows(cot, cotp, W)
    get_w2 = gather_weight(w2)
    step(get_img, get_w1)

    imgf[pl.ds(pl.multiple_of(rows * BAND, 16), BAND)] = img[...]
    cotp[pl.ds(pl.multiple_of(W + rows * BAND, 16), BAND)] = cot[...]
    for buffer in (actp, cotp, hp, pp):
        buffer[0:W] = jnp.zeros((W, buffer.shape[1]), BF16)
        buffer[W + PIX : 2 * W + PIX] = jnp.zeros((W, buffer.shape[1]), BF16)
    for basis, held in ((b1, bs1), (b2, bs2)):
        high, low = split(basis[...])
        held[0:RANK] = high
        held[RANK : 2 * RANK] = low
        held[2 * RANK : 3 * RANK] = high

    for _ in range(3):
        step(get_img, get_w1)
    step(get_cot, get_w2)
    step(get_img, get_w1)

    groups = group_matrix(C, lambda row: row)

    def img_rows(i):
        return imgf[pl.ds(pl.multiple_of(i * 16, 16), 16)].astype(F32)

    total = lax.fori_loop(0, PIX // 16, lambda i, acc: acc + fold8(img_rows(i)), jnp.zeros((8, C), F32))
    center = group_mean(total, groups)
    total = lax.fori_loop(
        0, PIX // 16, lambda i, acc: acc + fold8(jnp.square(img_rows(i) - center)), jnp.zeros((8, C), F32)
    )
    factor = lax.rsqrt(group_mean(total, groups) + EPS)

    def activate_rows(i, carry):
        u = (img_rows(i) - center) * factor
        actp[pl.ds(pl.multiple_of(W + i * 16, 16), 16)] = (u / (1.0 + jnp.exp(-u))).astype(BF16)
        return carry

    step(get_cot, get_w2)
    lax.fori_loop(0, PIX // 16, activate_rows, 0)
    step(get_w1)
    step(get_cot, get_w2)

    MT = 288

    def conv_tiles(source, weight, flip):
        def tile(i, carry):
            sums = None
            for p in range(3):
                first = (2 - p if flip else p) * W
                part = dot(
                    source[pl.ds(pl.multiple_of(first + i * MT, 16), MT)],
                    weight[:, p * Q : p * Q + Q],
                )
                sums = part if sums is None else sums + part
            s[pl.ds(pl.multiple_of(i * MT, 16), MT)] = sums
            return carry

        lax.fori_loop(0, PIX // MT, tile, 0)

    conv_tiles(actp, w1, False)
    step(get_cot, get_w2)

    col = lax.broadcasted_iota(jnp.int32, (W, 128), 0)
    lane = lax.broadcasted_iota(jnp.int32, (W, 128), 1)

    def row_at(h, base=0):
        return pl.ds(pl.multiple_of(base + h * W, 16), W)

    def from_left(v):
        return jnp.where(col >= 1, pltpu.roll(v, 1, 0), 0.0)

    def from_right(v):
        return jnp.where(col <= W - 2, pltpu.roll(v, W - 1, 0), 0.0)

    def col_sum(h, first, last):
        part = s[row_at(h)]
        main = first(part[:, 0:128]) + part[:, 128:256] + last(part[:, 256:384])
        rest = part[:, 384:512]
        rest = first(rest) + pltpu.roll(rest, 96, 1) + pltpu.roll(last(rest), 64, 1)
        return main, jnp.where(lane < 32, rest, 0.0)

    def spread_cols(buffer, h, main, rest, first, last):
        at = row_at(h, W)
        buffer[at, 0:128] = first(main).astype(BF16)
        buffer[at, 128:256] = main.astype(BF16)
        buffer[at, 256:384] = last(main).astype(BF16)
        packed = first(rest) + pltpu.roll(rest, 32, 1) + pltpu.roll(last(rest), 64, 1)
        buffer[at, 384:512] = packed.astype(BF16)

    def sum_x(h, acc):
        main, rest = col_sum(h, from_left, from_right)
        x[row_at(h), 0:128] = main
        x[row_at(h), 128:256] = rest
        return acc + fold8(jnp.concatenate([main, rest], axis=1))

    zero_acc = jnp.zeros((8, 256), F32)
    groups_x = group_matrix(256, lambda row: row)
    real = lax.broadcasted_iota(jnp.int32, (1, 256), 1) < RW
    center_x = group_mean(lax.fori_loop(0, H, sum_x, zero_acc), groups_x)

    def dev_x(h, acc):
        d = jnp.where(real, x[row_at(h)] - center_x, 0.0)
        return acc + fold8(d * d)

    factor_x = lax.rsqrt(group_mean(lax.fori_loop(0, H, dev_x, zero_acc), groups_x) + EPS)

    def hidden_rows(h, carry):
        u = jnp.where(real, (x[row_at(h)] - center_x) * factor_x, 0.0)
        x[row_at(h)] = u
        a = u / (1.0 + jnp.exp(-u))
        hidc[row_at(h)] = a.astype(BF16)
        spread_cols(hp, h, a[:, 0:128], a[:, 128:256], from_left, from_right)
        return carry

    lax.fori_loop(0, H, hidden_rows, 0)

    HALF = PIX // 2
    coef = dot_nt(hidc[...], bs2[0 : 2 * RANK])
    coef = coef[:, 0:RANK] + coef[:, RANK : 2 * RANK]
    hb[...] = jnp.concatenate([coef[0:HALF], coef[HALF:PIX]], axis=1).astype(BF16)
    hc0 = send(hb, hx, XN)
    step(get_cot, get_w2)

    def project_act(i, carry):
        a = actp[pl.ds(pl.multiple_of(W + i * 128, 16), 128)]
        c = dot_nt(a, bs1[0 : 2 * RANK])
        high, low = split(c[:, 0:RANK] + c[:, RANK : 2 * RANK])
        back = dot(jnp.concatenate([high, high, low], axis=1), bs1[...])
        left = (a.astype(F32) - back).astype(BF16)
        act_t[:, pl.ds(pl.multiple_of(i * 128, 128), 128)] = left.T
        return carry

    lax.fori_loop(0, PIX // 128, project_act, 0)

    hc0.wait_recv()
    hpair[z] = (hb[...].astype(F32) + hx[...].astype(F32)).astype(BF16)
    hcp = send(hpair.at[z], hpair.at[z], ZP)
    hcm = send(hpair.at[z], hpair.at[z], ZM)

    step(get_w2)
    conv_tiles(cotp, w2, True)

    hcp.wait_recv()
    hfp = send(hpair.at[zm, pl.ds(0, 288)], hpair.at[zm, pl.ds(0, 288)], ZP)
    hcm.wait_recv()
    hfm = send(hpair.at[zp, pl.ds(288, 288)], hpair.at[zp, pl.ds(288, 288)], ZM)

    def grad_rows(h, carry):
        acc, acc_u = carry
        main, rest = col_sum(h, from_right, from_left)
        hg = jnp.concatenate([main, rest], axis=1)
        u = x[row_at(h)]
        sig = 1.0 / (1.0 + jnp.exp(-u))
        d = hg * (sig * (1.0 + u * (1.0 - sig)))
        du[row_at(h)] = d
        return acc + fold8(d), acc_u + fold8(d * u)

    acc, acc_u = lax.fori_loop(0, H, grad_rows, (zero_acc, zero_acc))
    mean_d, mean_du = group_mean(acc, groups_x), group_mean(acc_u, groups_x)

    def pre_rows(h, carry):
        pre = factor_x * (du[row_at(h)] - mean_d - x[row_at(h)] * mean_du)
        pre = jnp.where(real, pre, 0.0)
        spread_cols(pp, h, pre[:, 0:128], pre[:, 128:256], from_right, from_left)
        return carry

    lax.fori_loop(0, H, pre_rows, 0)

    GT = 640

    def grad_tiles(n, left_t, buffer, first):
        def tile(i, carry):
            part = dot(left_t[pl.ds(pl.multiple_of(i * GT, 16), GT)], buffer[first : first + PIX])
            per = GT // (2 * DPW)
            gr[n, pl.ds(i * per, per)] = part.astype(BF16).reshape(per, 2, DPW, Q)
            return carry

        lax.fori_loop(0, C // GT, tile, 0)

    active = []

    def push(new=None):
        for one in list(active):
            if next(one, "done") == "done":
                active.remove(one)
        if new is not None:
            next(new)
            active.append(new)

    for p in range(3):
        grad_tiles(p, act_t, pp, (2 - p) * W)
        push(scatter_grad(p, g1, p))

    def conv_second(zz):
        sums = None
        for p in range(3):
            part = dot_nt(hp[pl.ds(pl.multiple_of(p * W + zz * 288, 16), 288)], w2[:, p * Q : p * Q + Q])
            sums = part if sums is None else sums + part
        o[zz] = sums.astype(BF16).reshape(2, BAND, C)

    def add_into(target, extra):
        return (target.astype(F32) + extra.astype(F32)).astype(BF16)

    conv_second(z2)
    oap, oam = send(o.at[z2, 0], qa.at[0], ZP), send(o.at[z2, 1], qa.at[1], ZM)
    push()
    conv_second(zp)
    conv_second(zm)
    push()
    oap.wait_recv()
    o[zp, 0] = add_into(o[zp, 0], qa[0])
    obp = send(o.at[zp], qb.at[0], ZP)
    oam.wait_recv()
    o[zm, 1] = add_into(o[zm, 1], qa[1])
    obm = send(o.at[zm], qb.at[1], ZM)
    conv_second(z)

    hfp.wait_recv()
    hfm.wait_recv()
    push()

    def project_hidden(h, carry):
        part = hpair[0, row_at(h)].astype(F32)
        for zz in range(1, 4):
            part = part + hpair[zz, row_at(h)].astype(F32)
        for side in range(2):
            high, low = split(part[:, side * RANK : side * RANK + RANK])
            back = dot(jnp.concatenate([high, high, low], axis=1), bs2[...])
            hh = h + side * (H // 2)
            left = hidc[row_at(hh)].astype(F32) - back
            spread_cols(pp, hh, left[:, 0:128], left[:, 128:256], from_left, from_right)
        return carry

    lax.fori_loop(0, H // 2, project_hidden, 0)

    def turn_cot(i, carry):
        cot_t[:, pl.ds(pl.multiple_of(i * 128, 128), 128)] = cotp[
            pl.ds(pl.multiple_of(W + i * 128, 16), 128)
        ].T
        return carry

    lax.fori_loop(0, PIX // 128, turn_cot, 0)

    def band(xx):
        return o[z, xx].astype(F32) + qb[0, xx].astype(F32) + qb[1, xx].astype(F32)

    odx = None
    for p in range(3):
        grad_tiles(3 + p, cot_t, pp, p * W)
        push(scatter_grad(3 + p, g2, p))
        if p == 1:
            obp.wait_recv()
            obm.wait_recv()
            qv[...] = band(1 - xl).astype(BF16)
            odx = send(qv, qd, XN)
    push()
    push()
    odx.wait_recv()
    out[...] = (img[...].astype(F32) + (band(xl) + qd[...].astype(F32))).astype(BF16)
    while active:
        push()
    for copy in pending:
        copy.wait_send()


def body(images, cotangent, first_weight, second_weight, first_basis, second_basis):
    mine = lax.dynamic_slice_in_dim(second_basis, lax.axis_index("rows") * RW, RW, 1)
    mine = jnp.pad(mine, ((0, 0), (0, 256 - RW)))
    vmem = lambda shape, kind=BF16: pltpu.VMEM(shape, kind)
    out, grad_one, grad_two = pl.pallas_call(
        kernel,
        out_shape=(
            jax.ShapeDtypeStruct((BAND, C), BF16),
            jax.ShapeDtypeStruct((9, DPW, RW), F32),
            jax.ShapeDtypeStruct((9, DPW, RW), F32),
        ),
        in_specs=[pl.BlockSpec(memory_space=pltpu.VMEM)] * 6,
        out_specs=[pl.BlockSpec(memory_space=pltpu.VMEM)] * 3,
        scratch_shapes=[
            vmem((PIX, C)),
            vmem((PIX + 2 * W, C)),
            vmem((C, K3)),
            vmem((C, K3)),
            vmem((PIX + 2 * W, C)),
            vmem((PIX, 256), F32),
            vmem((PIX, Q), F32),
            vmem((PIX, 256), F32),
            vmem((PIX, 256)),
            vmem((PIX + 2 * W, Q)),
            vmem((PIX + 2 * W, Q)),
            vmem((C, PIX)),
            vmem((C, PIX)),
            vmem((4, 2, BAND, C)),
            vmem((2, BAND, C)),
            vmem((2, 2, BAND, C)),
            vmem((BAND, C)),
            vmem((BAND, C)),
            vmem((PIX // 2, 128)),
            vmem((PIX // 2, 128)),
            vmem((4, PIX // 2, 128)),
            vmem((6, 8, 2, DPW, Q)),
            vmem((6, 8, DPW, Q)),
            vmem((6, 8, DPW, Q)),
            vmem((6, 2, DPW, Q)),
            vmem((6, 2, 2, DPW, Q)),
            vmem((6, DPW, Q)),
            vmem((6, DPW, Q)),
            vmem((3 * RANK, C)),
            vmem((3 * RANK, 256)),
            pltpu.SemaphoreType.DMA((N_SEM,)),
            pltpu.SemaphoreType.DMA((N_SEM,)),
        ],
        compiler_params=pltpu.CompilerParams(
            collective_id=0, has_side_effects=True, vmem_limit_bytes=66 * 1000 * 1000
        ),
    )(
        images.reshape(BAND, C),
        cotangent.reshape(BAND, C),
        first_weight.reshape(9, DPW, RW),
        second_weight.reshape(9, DPW, RW),
        first_basis,
        mine,
    )
    return (
        out.reshape(1, 3, W, C),
        grad_one.reshape(1, 1, 9, DPW * RW),
        grad_two.reshape(1, 1, 9, DPW * RW),
    )


def solution(mesh):
    return jax.shard_map(
        body,
        mesh=mesh,
        in_specs=(
            P("dp", "rows", None, None),
            P("dp", "rows", None, None),
            P("dp", "rows", None, None),
            P("dp", "rows", None, None),
            P(),
            P(),
        ),
        out_specs=(
            P("dp", "rows", None, None),
            P("dp", "rows", None, None),
            P("dp", "rows", None, None),
        ),
        check_vma=False,
    )
```

time: 794 us -> 154 us (0.19); the launches traced: 784 us -> 153 us
  waiting for transfers between devices: 558 us -> 0 us
  Pallas kernels: 0 us -> 142 us
  matrix products: 99.6 us -> 0 us
  local copies, waits for them, and re-layouts: 95.2 us -> 10.3 us
  other arithmetic: 16.1 us -> 0 us
  between operations: 14.5 us -> 0.67 us
    all_gather x4 -> x0, waiting for transfers between devices: 218 us -> none  [the longest x1 70.2 us: body(): lax.all_gather(images, 'rows', axis=1, tiled=True)]
    psum x2 -> x0, waiting for transfers between devices: 185 us -> none  [the longest x1 133 us: body(): lax.psum(coefficients(first_shard, basis_images).astype(jnp.bfloat16), 'dp')]
    pallas_call x0 -> x1, Pallas kernels: none -> 142 us  [body(): pl.pallas_call(kernel, out_shape=(jax.ShapeDtypeStruct((BAND, C), BF16),...]
    dot_general x49 -> x0, matrix products: 99.6 us -> none  [the longest x27 73.6 us: convolve(): jnp.einsum(form, window, kernel[row_tap, col_tap], preferred_element_type...]
    unnamed x11 -> x0, waiting for transfers between devices: 89.9 us -> none
    reduce_scatter x1 -> x0, waiting for transfers between devices: 65.6 us -> none  [body(): lax.psum_scatter(partial_sums.astype(jnp.bfloat16), 'rows', scatter_dimen...]
    unnamed x32 -> x9, local copies, waits for them, and re-layouts: 59.1 us -> 1.72 us
    reshape x4, local copies, waits for them, and re-layouts: 33.7 us -> 7.91 us  [the longest x1 2.8 us: body(): grad_one.reshape(1, 1, 9, DPW * RW)]
  transfers between devices with their start and end apart: 9 -> 0, of which waited for: 9 -> 0; matrix products, arithmetic and copies ran while one was open for 19% -> 0% of each run, Pallas kernels for 0% -> 0%
where the time goes in v1:
time: 154 us; the launch traced here: 153 us
  Pallas kernels  142 us (92%)
  local copies, waits for them, and re-layouts  10.3 us (7%)
    pallas_call x1, Pallas kernels, body(): pl.pallas_call(kernel, out_shape=(jax.ShapeDtypeStruct((BAND, C), BF16),...  142 us

profile of v1, /device:TPU:0, one launch (start us, length us, event | category | flops | bytes accessed | tf_op | source)
XLA Modules:
  0.0 152.6 jit_solution(15448281771830081048)
XLA Ops:
  0.6 0.0 copy-start
  0.6 1.0 copy-done
  1.6 0.1 constant_dynamic-slice_fusion
  1.7 0.6 pad.4.b2
  2.3 0.0 copy-start.2
  2.3 2.3 %reshape.29.w1r = bf16[9,80,160]{2,1,0:T(8,128)(2,1)} reshape(bf16[1,1,9,12800]{3,2,1,0:T(8,128)(2,1)} %param.8) | data formatting | bytes 460800 | tf_op jit(solution)/shard_map/reshape | solution.py:539
  4.6 0.0 copy-done.2
  4.6 1.2 reshape.30.w2r
  5.8 141.6 %shard_map.85 = (bf16[144,1280]{1,0:T(8,128)(2,1)}, f32[9,80,160]{2,1,0:T(8,128)}, f32[9,80,160]{2,1,0:T(8,128)}) custom-call(bf16[144,1280]{1,0:T(8,128)(2,1)} %bitcast.3, bf16[144,1280]{1,0:T(8,128)(2,1)} %bitcast.4, bf16[9,80,160]{2,1,0:T(8,128)(2,1)} %reshape.29.w1r, bf16[9,80,160]{2,1,0:T(8,128)(2,1)} %reshape.30.w2r, f32[64,1280]{1,0:T(8,128)} %b1.1, ...), custom_call_target="tpu_custom_call" | custom-call | tf_op jit(solution)/shard_map/pallas_call | solution.py:490
  147.4 0.0 copy-start.1
  147.5 2.8 %reshape.34 = f32[1,1,9,12800]{3,1,2,0:T(1,128)} reshape(f32[9,80,160]{2,1,0:T(8,128)} %get-tuple-element.7) | data formatting | bytes 921600 | tf_op jit(solution)/shard_map/reshape | solution.py:546
  150.3 0.0 copy-done.1
  150.3 0.0 copy-start.3
  150.3 1.6 %reshape.35 = f32[1,1,9,12800]{3,1,2,0:T(1,128)} reshape(f32[9,80,160]{2,1,0:T(8,128)S(1)} %copy-done.1) | data formatting | bytes 921600 | tf_op jit(solution)/shard_map/reshape | solution.py:547
  151.9 0.0 copy-done.3
  151.9 0.7 copy.14
Async XLA Ops:
  0.6 1.0 copy-start
  2.3 2.3 %copy-start.2 = (bf16[1,1,9,12800]{3,2,1,0:T(8,128)(2,1)S(1)}, bf16[1,1,9,12800]{3,2,1,0:T(8,128)(2,1)}, u32[]{:S(2)}) copy-start(bf16[1,1,9,12800]{3,2,1,0:T(8,128)(2,1)} %param.9) | copy-start | bytes 691204
  147.4 2.8 %copy-start.1 = (f32[9,80,160]{2,1,0:T(8,128)S(1)}, f32[9,80,160]{2,1,0:T(8,128)}, u32[]{:S(2)}) copy-start(f32[9,80,160]{2,1,0:T(8,128)} %get-tuple-element.8) | copy-start | bytes 1382404
  150.3 1.6 %copy-start.3 = (bf16[144,1280]{1,0:T(8,128)(2,1)S(1)}, bf16[144,1280]{1,0:T(8,128)(2,1)}, u32[]{:S(2)}) copy-start(bf16[144,1280]{1,0:T(8,128)(2,1)} %get-tuple-element.6) | copy-start | bytes 1105924

commit v2 on v1

--- a/solution.py
+++ b/solution.py
@@ -23,7 +23,9 @@
 BF16 = jnp.bfloat16
 MESH = pl.DeviceIdType.MESH
 HIGH = lax.Precision.HIGHEST
-N_SEM = 104
+N_SEM = 120
+PART = 96
+AT = 384
 
 
 def dot(a, b):
@@ -65,7 +67,7 @@
 def kernel(
     img, cot, w1r, w2r, b1, b2, out, g1, g2,
     imgf, cotp, w1, w2, actp, x, s, du, hidc, hp, pp, act_t, cot_t,
-    o, qa, qb, qd, qv, hb, hx, hpair, gr, gc, gt, ga, gb, gd, gu, bs1, bs2,
+    o, qa, qb, qd, qv, hb, hx, hpair, gr, gc, gt, ga, gb, gd, gu, bs1, bs2, means, squares,
     ssem, rsem,
 ):
     dp = lax.axis_index("dp")
@@ -94,67 +96,99 @@
         pending.append(copy)
         return copy
 
+    def pass_on(piece, device):
+        return send(piece, piece, device)
+
     def gather_rows(src, full, base):
-        def at(zz, xx, low=0, size=BAND):
-            return full.at[pl.ds(pl.multiple_of(base + (zz * 2 + xx) * BAND + low, 16), size)]
-
-        def pass_on(piece, device):
-            return send(piece, piece, device)
-
-        own = at(z, xl)
-        cx, cp, cm = send(src, own, XN), send(src, own, ZP), send(src, own, ZM)
-        yield
-        cx.wait_recv()
-        ep, em = pass_on(at(z, 1 - xl), ZP), pass_on(at(z, 1 - xl), ZM)
-        yield
-        cp.wait_recv()
-        fp = pass_on(at(zm, xl, 0, 80), ZP)
-        cm.wait_recv()
-        fm = pass_on(at(zp, xl, 80, 64), ZM)
-        yield
-        ep.wait_recv()
-        hp_ = pass_on(at(zm, 1 - xl, 0, 80), ZP)
-        em.wait_recv()
-        hm_ = pass_on(at(zp, 1 - xl, 80, 64), ZM)
-        yield
-        for copy in (fp, fm, hp_, hm_):
+        one, two = (0, 80), (80, 64)
+
+        def at(zz, xx, part):
+            return full.at[pl.ds(pl.multiple_of(base + (zz * 2 + xx) * BAND + part[0], 16), part[1])]
+
+        def own(part, device):
+            return send(src.at[pl.ds(part[0], part[1])], at(z, xl, part), device)
+
+        cx = own(one, XN), own(two, XN)
+        yield
+        cp1, cm2, cp2, cm1 = own(one, ZP), own(two, ZM), own(two, ZP), own(one, ZM)
+        yield
+        cp1.wait_recv()
+        fp = pass_on(at(zm, xl, one), ZP)
+        cm2.wait_recv()
+        fm = pass_on(at(zp, xl, two), ZM)
+        yield
+        cx[0].wait_recv()
+        ep1, em1 = pass_on(at(z, 1 - xl, one), ZP), pass_on(at(z, 1 - xl, one), ZM)
+        yield
+        cx[1].wait_recv()
+        ep2, em2 = pass_on(at(z, 1 - xl, two), ZP), pass_on(at(z, 1 - xl, two), ZM)
+        yield
+        cp2.wait_recv()
+        cm1.wait_recv()
+        yield
+        ep1.wait_recv()
+        hp_ = pass_on(at(zm, 1 - xl, one), ZP)
+        em2.wait_recv()
+        hm_ = pass_on(at(zp, 1 - xl, two), ZM)
+        yield
+        for copy in (fp, fm, ep2, em1):
             copy.wait_recv()
         yield
+        hp_.wait_recv()
+        hm_.wait_recv()
+        yield
 
     def gather_weight(full):
-        def at(yy, hh, low=0, size=DPW):
-            return full.at[pl.ds(pl.multiple_of(((yy * 2 + hh) * 2 + core) * DPW + low, 16), size)]
-
-        def pass_on(piece, device):
-            return send(piece, piece, device)
-
-        own = at(y, xh)
-        ax, ap, am, ac = (pass_on(own, device) for device in (XH, YP, YM, CN))
-        yield
-        ax.wait_recv()
-        bp, bm, bc = (pass_on(at(y, 1 - xh), device) for device in (YP, YM, CN))
-        yield
-        ap.wait_recv()
-        fp, fc = pass_on(at(ym, xh, 0, 48), YP), pass_on(at(ym, xh), CN)
-        am.wait_recv()
-        fm, fd = pass_on(at(yp, xh, 48, 32), YM), pass_on(at(yp, xh), CN)
-        yield
-        bp.wait_recv()
-        hp_, hc = pass_on(at(ym, 1 - xh, 0, 48), YP), pass_on(at(ym, 1 - xh), CN)
-        bm.wait_recv()
-        hm_, hd = pass_on(at(yp, 1 - xh, 48, 32), YM), pass_on(at(yp, 1 - xh), CN)
-        yield
+        one, two, both = (0, 48), (48, 32), (0, DPW)
+
+        def at(yy, hh, part=both):
+            return full.at[pl.ds(pl.multiple_of(((yy * 2 + hh) * 2 + core) * DPW + part[0], 16), part[1])]
+
         last = []
+
+        def to_core(yy, hh):
+            last.append(pass_on(at(yy, hh), CN))
+
+        ax = pass_on(at(y, xh, one), XH), pass_on(at(y, xh, two), XH)
+        yield
+        ap1, am2 = pass_on(at(y, xh, one), YP), pass_on(at(y, xh, two), YM)
+        ap2, am1 = pass_on(at(y, xh, two), YP), pass_on(at(y, xh, one), YM)
+        to_core(y, xh)
+        yield
+        ap1.wait_recv()
+        fp = pass_on(at(ym, xh, one), YP)
+        am2.wait_recv()
+        fm = pass_on(at(yp, xh, two), YM)
+        yield
+        ax[0].wait_recv()
+        bp1, bm1 = pass_on(at(y, 1 - xh, one), YP), pass_on(at(y, 1 - xh, one), YM)
+        ax[1].wait_recv()
+        bp2, bm2 = pass_on(at(y, 1 - xh, two), YP), pass_on(at(y, 1 - xh, two), YM)
+        to_core(y, 1 - xh)
+        yield
+        ap2.wait_recv()
+        to_core(ym, xh)
+        am1.wait_recv()
+        to_core(yp, xh)
+        yield
+        bp1.wait_recv()
+        hp_ = pass_on(at(ym, 1 - xh, one), YP)
+        bm2.wait_recv()
+        hm_ = pass_on(at(yp, 1 - xh, two), YM)
+        yield
+        bp2.wait_recv()
+        to_core(ym, 1 - xh)
+        bm1.wait_recv()
+        to_core(yp, 1 - xh)
         fp.wait_recv()
-        last.append(pass_on(at(y2, xh, 0, 48), CN))
         fm.wait_recv()
-        last.append(pass_on(at(y2, xh, 48, 32), CN))
+        to_core(y2, xh)
+        yield
         hp_.wait_recv()
-        last.append(pass_on(at(y2, 1 - xh, 0, 48), CN))
         hm_.wait_recv()
-        last.append(pass_on(at(y2, 1 - xh, 48, 32), CN))
-        yield
-        for copy in [ac, bc, fc, fd, hc, hd] + last:
+        to_core(y2, 1 - xh)
+        yield
+        for copy in last:
             copy.wait_recv()
         yield
 
@@ -197,6 +231,10 @@
     def step(*work):
         for one in work:
             next(one)
+
+    barrier = pltpu.get_barrier_semaphore()
+    for device in (ZP, ZM, XN, YP, YM, XH, CN):
+        pl.semaphore_signal(barrier, inc=1, device_id=device, device_id_type=MESH)
 
     for raw, full in ((w1r, w1), (w2r, w2)):
         mine_at = pl.ds(pl.multiple_of(dp * DPW, 16), DPW)
@@ -211,16 +249,13 @@
                 rest = rest + (tail if q == 0 else pltpu.roll(tail, 32 * q, 1))
             full[mine_at, p * Q + 384 : p * Q + 512] = rest.astype(BF16)
 
-    barrier = pltpu.get_barrier_semaphore()
-    for device in (ZP, ZM, XN, YP, YM, XH, CN):
-        pl.semaphore_signal(barrier, inc=1, device_id=device, device_id_type=MESH)
     pl.semaphore_wait(barrier, 7)
 
     get_img = gather_rows(img, imgf, 0)
     get_w1 = gather_weight(w1)
     get_cot = gather_rows(cot, cotp, W)
     get_w2 = gather_weight(w2)
-    step(get_img, get_w1)
+    step(get_w1, get_img, get_img, get_w1, get_w2, get_cot)
 
     imgf[pl.ds(pl.multiple_of(rows * BAND, 16), BAND)] = img[...]
     cotp[pl.ds(pl.multiple_of(W + rows * BAND, 16), BAND)] = cot[...]
@@ -233,36 +268,57 @@
         held[RANK : 2 * RANK] = low
         held[2 * RANK : 3 * RANK] = high
 
-    for _ in range(3):
-        step(get_img, get_w1)
-    step(get_cot, get_w2)
-    step(get_img, get_w1)
+    def band_stats(slot, zz, xx):
+        base = (zz * 2 + xx) * BAND
+
+        def rows_of(i):
+            return imgf[pl.ds(pl.multiple_of(base + i * 16, 16), 16)].astype(F32)
+
+        total = lax.fori_loop(0, BAND // 16, lambda i, acc: acc + fold8(rows_of(i)), jnp.zeros((8, C), F32))
+        mean = jnp.sum(total, axis=0, keepdims=True) * (1.0 / BAND)
+        means[slot : slot + 1] = mean
+        squares[...] = lax.fori_loop(
+            0, BAND // 16, lambda i, acc: acc + fold8(jnp.square(rows_of(i) - mean)), squares[...]
+        )
+
+    squares[...] = jnp.zeros((8, C), F32)
+    band_stats(0, z, xl)
+    step(get_w1, get_img, get_w1, get_img, get_img)
+    band_stats(1, z, 1 - xl)
+    step(get_w1, get_w1, get_img)
+    step(get_w2)
+    band_stats(2, zm, xl)
+    band_stats(3, zp, xl)
+    step(get_img, get_cot)
+    step(get_w1, get_w1)
+    step(get_img)
+    band_stats(4, z2, xl)
+    band_stats(5, zm, 1 - xl)
+    band_stats(6, zp, 1 - xl)
+    step(get_w2, get_w2)
+    step(get_img)
+    band_stats(7, z2, 1 - xl)
 
     groups = group_matrix(C, lambda row: row)
+    center = group_mean(means[...] * BAND, groups)
+    total = squares[...] + BAND * jnp.square(means[...] - center)
+    factor = lax.rsqrt(group_mean(total, groups) + EPS)
 
     def img_rows(i):
         return imgf[pl.ds(pl.multiple_of(i * 16, 16), 16)].astype(F32)
-
-    total = lax.fori_loop(0, PIX // 16, lambda i, acc: acc + fold8(img_rows(i)), jnp.zeros((8, C), F32))
-    center = group_mean(total, groups)
-    total = lax.fori_loop(
-        0, PIX // 16, lambda i, acc: acc + fold8(jnp.square(img_rows(i) - center)), jnp.zeros((8, C), F32)
-    )
-    factor = lax.rsqrt(group_mean(total, groups) + EPS)
 
     def activate_rows(i, carry):
         u = (img_rows(i) - center) * factor
         actp[pl.ds(pl.multiple_of(W + i * 16, 16), 16)] = (u / (1.0 + jnp.exp(-u))).astype(BF16)
         return carry
 
-    step(get_cot, get_w2)
     lax.fori_loop(0, PIX // 16, activate_rows, 0)
+    step(get_cot, get_cot, get_cot, get_w2, get_w2)
     step(get_w1)
-    step(get_cot, get_w2)
 
     MT = 288
 
-    def conv_tiles(source, weight, flip):
+    def conv_tiles(source, weight, flip, begin=0, end=PIX // MT):
         def tile(i, carry):
             sums = None
             for p in range(3):
@@ -275,22 +331,22 @@
             s[pl.ds(pl.multiple_of(i * MT, 16), MT)] = sums
             return carry
 
-        lax.fori_loop(0, PIX // MT, tile, 0)
+        lax.fori_loop(begin, end, tile, 0)
 
     conv_tiles(actp, w1, False)
-    step(get_cot, get_w2)
-
-    col = lax.broadcasted_iota(jnp.int32, (W, 128), 0)
-    lane = lax.broadcasted_iota(jnp.int32, (W, 128), 1)
+    step(get_w2, get_cot, get_w2)
+
+    col = lax.broadcasted_iota(jnp.int32, (PART // W, W, 128), 1).reshape(PART, 128)
+    lane = lax.broadcasted_iota(jnp.int32, (PART, 128), 1)
 
     def row_at(h, base=0):
-        return pl.ds(pl.multiple_of(base + h * W, 16), W)
+        return pl.ds(pl.multiple_of(base + h * PART, 16), PART)
 
     def from_left(v):
         return jnp.where(col >= 1, pltpu.roll(v, 1, 0), 0.0)
 
     def from_right(v):
-        return jnp.where(col <= W - 2, pltpu.roll(v, W - 1, 0), 0.0)
+        return jnp.where(col <= W - 2, pltpu.roll(v, PART - 1, 0), 0.0)
 
     def col_sum(h, first, last):
         part = s[row_at(h)]
@@ -316,13 +372,13 @@
     zero_acc = jnp.zeros((8, 256), F32)
     groups_x = group_matrix(256, lambda row: row)
     real = lax.broadcasted_iota(jnp.int32, (1, 256), 1) < RW
-    center_x = group_mean(lax.fori_loop(0, H, sum_x, zero_acc), groups_x)
+    center_x = group_mean(lax.fori_loop(0, PIX // PART, sum_x, zero_acc), groups_x)
 
     def dev_x(h, acc):
         d = jnp.where(real, x[row_at(h)] - center_x, 0.0)
         return acc + fold8(d * d)
 
-    factor_x = lax.rsqrt(group_mean(lax.fori_loop(0, H, dev_x, zero_acc), groups_x) + EPS)
+    factor_x = lax.rsqrt(group_mean(lax.fori_loop(0, PIX // PART, dev_x, zero_acc), groups_x) + EPS)
 
     def hidden_rows(h, carry):
         u = jnp.where(real, (x[row_at(h)] - center_x) * factor_x, 0.0)
@@ -332,38 +388,115 @@
         spread_cols(hp, h, a[:, 0:128], a[:, 128:256], from_left, from_right)
         return carry
 
-    lax.fori_loop(0, H, hidden_rows, 0)
+    lax.fori_loop(0, PIX // PART, hidden_rows, 0)
 
     HALF = PIX // 2
     coef = dot_nt(hidc[...], bs2[0 : 2 * RANK])
     coef = coef[:, 0:RANK] + coef[:, RANK : 2 * RANK]
     hb[...] = jnp.concatenate([coef[0:HALF], coef[HALF:PIX]], axis=1).astype(BF16)
     hc0 = send(hb, hx, XN)
-    step(get_cot, get_w2)
 
     def project_act(i, carry):
-        a = actp[pl.ds(pl.multiple_of(W + i * 128, 16), 128)]
+        a = actp[pl.ds(pl.multiple_of(W + i * AT, 16), AT)]
         c = dot_nt(a, bs1[0 : 2 * RANK])
         high, low = split(c[:, 0:RANK] + c[:, RANK : 2 * RANK])
         back = dot(jnp.concatenate([high, high, low], axis=1), bs1[...])
         left = (a.astype(F32) - back).astype(BF16)
-        act_t[:, pl.ds(pl.multiple_of(i * 128, 128), 128)] = left.T
+        act_t[:, pl.ds(pl.multiple_of(i * AT, 128), AT)] = left.T
         return carry
 
-    lax.fori_loop(0, PIX // 128, project_act, 0)
-
+    project_act(0, 0)
     hc0.wait_recv()
     hpair[z] = (hb[...].astype(F32) + hx[...].astype(F32)).astype(BF16)
     hcp = send(hpair.at[z], hpair.at[z], ZP)
     hcm = send(hpair.at[z], hpair.at[z], ZM)
+    step(get_cot)
+    project_act(1, 0)
+    project_act(2, 0)
+
+    GT = 640
+
+    def grad_tiles(n, left_t, buffer, first):
+        def tile(i, carry):
+            part = dot(left_t[pl.ds(pl.multiple_of(i * GT, 16), GT)], buffer[first : first + PIX])
+            per = GT // (2 * DPW)
+            gr[n, pl.ds(i * per, per)] = part.astype(BF16).reshape(per, 2, DPW, Q)
+            return carry
+
+        lax.fori_loop(0, C // GT, tile, 0)
+
+    chunks = [scatter_grad(3 + p, g2, p) for p in range(3)] + [scatter_grad(p, g1, p) for p in range(3)]
+
+    def move(*which):
+        for one in which:
+            next(chunks[one])
+
+    def conv_second(zz):
+        sums = None
+        for p in range(3):
+            part = dot_nt(hp[pl.ds(pl.multiple_of(p * W + zz * 288, 16), 288)], w2[:, p * Q : p * Q + Q])
+            sums = part if sums is None else sums + part
+        o[zz] = sums.astype(BF16).reshape(2, BAND, C)
+
+    def add_into(target, extra):
+        return (target.astype(F32) + extra.astype(F32)).astype(BF16)
 
     step(get_w2)
-    conv_tiles(cotp, w2, True)
-
+    conv_second(z2)
     hcp.wait_recv()
     hfp = send(hpair.at[zm, pl.ds(0, 288)], hpair.at[zm, pl.ds(0, 288)], ZP)
     hcm.wait_recv()
     hfm = send(hpair.at[zp, pl.ds(288, 288)], hpair.at[zp, pl.ds(288, 288)], ZM)
+    oap, oam = send(o.at[z2, 0], qa.at[0], ZP), send(o.at[z2, 1], qa.at[1], ZM)
+
+    conv_second(zp)
+    hfp.wait_recv()
+    hfm.wait_recv()
+
+    def project_hidden(h, carry):
+        part = hpair[0, row_at(h)].astype(F32)
+        for zz in range(1, 4):
+            part = part + hpair[zz, row_at(h)].astype(F32)
+        for side in range(2):
+            high, low = split(part[:, side * RANK : side * RANK + RANK])
+            back = dot(jnp.concatenate([high, high, low], axis=1), bs2[...])
+            hh = h + side * (HALF // PART)
+            left = hidc[row_at(hh)].astype(F32) - back
+            spread_cols(pp, hh, left[:, 0:128], left[:, 128:256], from_left, from_right)
+        return carry
+
+    lax.fori_loop(0, HALF // PART, project_hidden, 0)
+
+    step(get_cot, get_cot)
+
+    def turn_cot(i, carry):
+        cot_t[:, pl.ds(pl.multiple_of(i * 128, 128), 128)] = cotp[
+            pl.ds(pl.multiple_of(W + i * 128, 16), 128)
+        ].T
+        return carry
+
+    lax.fori_loop(0, PIX // 128, turn_cot, 0)
+
+    grad_tiles(3, cot_t, pp, 0)
+    move(0)
+    grad_tiles(4, cot_t, pp, W)
+    move(1, 0)
+    grad_tiles(5, cot_t, pp, 2 * W)
+    move(2, 1)
+    conv_second(zm)
+    move(2)
+    oap.wait_recv()
+    o[zp, 0] = add_into(o[zp, 0], qa[0])
+    obp = send(o.at[zp], qb.at[0], ZP)
+    oam.wait_recv()
+    o[zm, 1] = add_into(o[zm, 1], qa[1])
+    obm = send(o.at[zm], qb.at[1], ZM)
+    move(0)
+
+    conv_tiles(cotp, w2, True, 0, 2)
+    move(1)
+    conv_tiles(cotp, w2, True, 2, 4)
+    move(2)
 
     def grad_rows(h, carry):
         acc, acc_u = carry
@@ -375,7 +508,8 @@
         du[row_at(h)] = d
         return acc + fold8(d), acc_u + fold8(d * u)
 
-    acc, acc_u = lax.fori_loop(0, H, grad_rows, (zero_acc, zero_acc))
+    acc, acc_u = lax.fori_loop(0, PIX // PART, grad_rows, (zero_acc, zero_acc))
+    move(0)
     mean_d, mean_du = group_mean(acc, groups_x), group_mean(acc_u, groups_x)
 
     def pre_rows(h, carry):
@@ -384,101 +518,30 @@
         spread_cols(pp, h, pre[:, 0:128], pre[:, 128:256], from_right, from_left)
         return carry
 
-    lax.fori_loop(0, H, pre_rows, 0)
-
-    GT = 640
-
-    def grad_tiles(n, left_t, buffer, first):
-        def tile(i, carry):
-            part = dot(left_t[pl.ds(pl.multiple_of(i * GT, 16), GT)], buffer[first : first + PIX])
-            per = GT // (2 * DPW)
-            gr[n, pl.ds(i * per, per)] = part.astype(BF16).reshape(per, 2, DPW, Q)
-            return carry
-
-        lax.fori_loop(0, C // GT, tile, 0)
-
-    active = []
-
-    def push(new=None):
-        for one in list(active):
-            if next(one, "done") == "done":
-                active.remove(one)
-        if new is not None:
-            next(new)
-            active.append(new)
-
-    for p in range(3):
-        grad_tiles(p, act_t, pp, (2 - p) * W)
-        push(scatter_grad(p, g1, p))
-
-    def conv_second(zz):
-        sums = None
-        for p in range(3):
-            part = dot_nt(hp[pl.ds(pl.multiple_of(p * W + zz * 288, 16), 288)], w2[:, p * Q : p * Q + Q])
-            sums = part if sums is None else sums + part
-        o[zz] = sums.astype(BF16).reshape(2, BAND, C)
-
-    def add_into(target, extra):
-        return (target.astype(F32) + extra.astype(F32)).astype(BF16)
-
-    conv_second(z2)
-    oap, oam = send(o.at[z2, 0], qa.at[0], ZP), send(o.at[z2, 1], qa.at[1], ZM)
-    push()
-    conv_second(zp)
-    conv_second(zm)
-    push()
-    oap.wait_recv()
-    o[zp, 0] = add_into(o[zp, 0], qa[0])
-    obp = send(o.at[zp], qb.at[0], ZP)
-    oam.wait_recv()
-    o[zm, 1] = add_into(o[zm, 1], qa[1])
-    obm = send(o.at[zm], qb.at[1], ZM)
-    conv_second(z)
-
-    hfp.wait_recv()
-    hfm.wait_recv()
-    push()
-
-    def project_hidden(h, carry):
-        part = hpair[0, row_at(h)].astype(F32)
-        for zz in range(1, 4):
-            part = part + hpair[zz, row_at(h)].astype(F32)
-        for side in range(2):
-            high, low = split(part[:, side * RANK : side * RANK + RANK])
-            back = dot(jnp.concatenate([high, high, low], axis=1), bs2[...])
-            hh = h + side * (H // 2)
-            left = hidc[row_at(hh)].astype(F32) - back
-            spread_cols(pp, hh, left[:, 0:128], left[:, 128:256], from_left, from_right)
-        return carry
-
-    lax.fori_loop(0, H // 2, project_hidden, 0)
-
-    def turn_cot(i, carry):
-        cot_t[:, pl.ds(pl.multiple_of(i * 128, 128), 128)] = cotp[
-            pl.ds(pl.multiple_of(W + i * 128, 16), 128)
-        ].T
-        return carry
-
-    lax.fori_loop(0, PIX // 128, turn_cot, 0)
+    lax.fori_loop(0, PIX // PART, pre_rows, 0)
+
+    move(1)
 
     def band(xx):
         return o[z, xx].astype(F32) + qb[0, xx].astype(F32) + qb[1, xx].astype(F32)
 
-    odx = None
-    for p in range(3):
-        grad_tiles(3 + p, cot_t, pp, p * W)
-        push(scatter_grad(3 + p, g2, p))
-        if p == 1:
-            obp.wait_recv()
-            obm.wait_recv()
-            qv[...] = band(1 - xl).astype(BF16)
-            odx = send(qv, qd, XN)
-    push()
-    push()
+    grad_tiles(0, act_t, pp, 2 * W)
+    move(3)
+    grad_tiles(1, act_t, pp, W)
+    move(4, 3)
+    grad_tiles(2, act_t, pp, 0)
+    move(5, 4, 2)
+    conv_second(z)
+    move(5, 3)
+    obp.wait_recv()
+    obm.wait_recv()
+    qv[...] = band(1 - xl).astype(BF16)
+    odx = send(qv, qd, XN)
+
+    move(4, 5, 0, 1, 2, 3, 4, 5)
     odx.wait_recv()
     out[...] = (img[...].astype(F32) + (band(xl) + qd[...].astype(F32))).astype(BF16)
-    while active:
-        push()
+    move(3, 4, 5)
     for copy in pending:
         copy.wait_send()
 
@@ -527,6 +590,8 @@
             vmem((6, DPW, Q)),
             vmem((3 * RANK, C)),
             vmem((3 * RANK, 256)),
+            vmem((8, C), F32),
+            vmem((8, C), F32),
             pltpu.SemaphoreType.DMA((N_SEM,)),
             pltpu.SemaphoreType.DMA((N_SEM,)),
         ],

time: 154 us -> 133 us (0.86)
  Pallas kernels: 142 us -> 121 us
    pallas_call x1, Pallas kernels: 142 us -> 121 us  [body(): pl.pallas_call(kernel, out_shape=(jax.ShapeDtypeStruct((BAND, C), BF16),...]
where the time goes in v2:
time: 133 us; the launch traced here: 132 us
  Pallas kernels  121 us (91%)
  local copies, waits for them, and re-layouts  10.3 us (8%)
    pallas_call x1, Pallas kernels, body(): pl.pallas_call(kernel, out_shape=(jax.ShapeDtypeStruct((BAND, C), BF16),...  121 us
    reshape x1, local copies, waits for them, and re-layouts, body(): grad_one.reshape(1, 1, 9, DPW * RW)  2.8 us

profile of v2, /device:TPU:0, one launch (start us, length us, event | category | flops | bytes accessed | tf_op | source)
XLA Modules:
  0.0 132.2 jit_solution(16603795247555276075)
XLA Ops:
  0.6 0.0 copy-start
  0.6 1.0 copy-done
  1.6 0.1 constant_dynamic-slice_fusion
  1.7 0.6 pad.4.b2
  2.3 0.0 copy-start.2
  2.3 2.3 %reshape.29.w1r = bf16[9,80,160]{2,1,0:T(8,128)(2,1)} reshape(bf16[1,1,9,12800]{3,2,1,0:T(8,128)(2,1)} %param.8) | data formatting | bytes 460800 | tf_op jit(solution)/shard_map/reshape | solution.py:604
  4.6 0.0 copy-done.2
  4.6 1.2 reshape.30.w2r
  5.8 121.2 %shard_map.85 = (bf16[144,1280]{1,0:T(8,128)(2,1)}, f32[9,80,160]{2,1,0:T(8,128)}, f32[9,80,160]{2,1,0:T(8,128)}) custom-call(bf16[144,1280]{1,0:T(8,128)(2,1)} %bitcast.3, bf16[144,1280]{1,0:T(8,128)(2,1)} %bitcast.4, bf16[9,80,160]{2,1,0:T(8,128)(2,1)} %reshape.29.w1r, bf16[9,80,160]{2,1,0:T(8,128)(2,1)} %reshape.30.w2r, f32[64,1280]{1,0:T(8,128)} %b1.1, ...), custom_call_target="tpu_custom_call" | custom-call | tf_op jit(solution)/shard_map/pallas_call | solution.py:553
  127.0 0.0 copy-start.1
  127.0 2.8 %reshape.34 = f32[1,1,9,12800]{3,1,2,0:T(1,128)} reshape(f32[9,80,160]{2,1,0:T(8,128)} %get-tuple-element.7) | data formatting | bytes 921600 | tf_op jit(solution)/shard_map/reshape | solution.py:611
  129.8 0.0 copy-done.1
  129.8 0.0 copy-start.3
  129.8 1.6 %reshape.35 = f32[1,1,9,12800]{3,1,2,0:T(1,128)} reshape(f32[9,80,160]{2,1,0:T(8,128)S(1)} %copy-done.1) | data formatting | bytes 921600 | tf_op jit(solution)/shard_map/reshape | solution.py:612
  131.4 0.0 copy-done.3
  131.4 0.7 copy.14
Async XLA Ops:
  0.6 1.0 copy-start
  2.3 2.3 %copy-start.2 = (bf16[1,1,9,12800]{3,2,1,0:T(8,128)(2,1)S(1)}, bf16[1,1,9,12800]{3,2,1,0:T(8,128)(2,1)}, u32[]{:S(2)}) copy-start(bf16[1,1,9,12800]{3,2,1,0:T(8,128)(2,1)} %param.9) | copy-start | bytes 691204
  127.0 2.8 %copy-start.1 = (f32[9,80,160]{2,1,0:T(8,128)S(1)}, f32[9,80,160]{2,1,0:T(8,128)}, u32[]{:S(2)}) copy-start(f32[9,80,160]{2,1,0:T(8,128)} %get-tuple-element.8) | copy-start | bytes 1382404
  129.8 1.6 %copy-start.3 = (bf16[144,1280]{1,0:T(8,128)(2,1)S(1)}, bf16[144,1280]{1,0:T(8,128)(2,1)}, u32[]{:S(2)}) copy-start(bf16[144,1280]{1,0:T(8,128)(2,1)} %get-tuple-element.6) | copy-start | bytes 1105924

commit v3 on v2

--- a/solution.py
+++ b/solution.py
@@ -23,8 +23,8 @@
 BF16 = jnp.bfloat16
 MESH = pl.DeviceIdType.MESH
 HIGH = lax.Precision.HIGHEST
-N_SEM = 120
-PART = 96
+N_SEM = 124
+PART = 288
 AT = 384
 
 
@@ -67,7 +67,7 @@
 def kernel(
     img, cot, w1r, w2r, b1, b2, out, g1, g2,
     imgf, cotp, w1, w2, actp, x, s, du, hidc, hp, pp, act_t, cot_t,
-    o, qa, qb, qd, qv, hb, hx, hpair, gr, gc, gt, ga, gb, gd, gu, bs1, bs2, means, squares,
+    o, qa, qb, qd, qv, hb, hx, hpair, gr, gc, gt, ga, gb, gd, gu, bs1, bs2, means, squares, flat,
     ssem, rsem,
 ):
     dp = lax.axis_index("dp")
@@ -138,6 +138,48 @@
         hm_.wait_recv()
         yield
 
+    def gather_rows_late(src, full, base):
+        one, two, low, high = (0, 80), (80, 64), (0, 48), (48, 32)
+
+        def at(zz, xx, part):
+            return full.at[pl.ds(pl.multiple_of(base + (zz * 2 + xx) * BAND + part[0], 16), part[1])]
+
+        def own(part, device):
+            return send(src.at[pl.ds(part[0], part[1])], at(z, xl, part), device)
+
+        cx = own(one, XN), own(two, XN)
+        yield
+        cp1, cm2, cp2, cm1 = own(one, ZP), own(two, ZM), own(two, ZP), own(one, ZM)
+        yield
+        cp1.wait_recv()
+        fp = pass_on(at(zm, xl, one), ZP)
+        cm2.wait_recv()
+        fm = pass_on(at(zp, xl, two), ZM)
+        gp = pass_on(at(zp, xl, two), XN)
+        yield
+        cx[0].wait_recv()
+        ep, em = pass_on(at(z, 1 - xl, one), ZP), pass_on(at(z, 1 - xl, one), ZM)
+        yield
+        cp2.wait_recv()
+        gm = pass_on(at(zm, xl, two), XN)
+        yield
+        cx[1].wait_recv()
+        cm1.wait_recv()
+        yield
+        ep.wait_recv()
+        hp_ = pass_on(at(zm, 1 - xl, low), ZP)
+        em.wait_recv()
+        hm_ = pass_on(at(zp, 1 - xl, high), ZM)
+        fm.wait_recv()
+        gf = pass_on(at(z2, xl, two), XN)
+        yield
+        for copy in (fp, gp, gm):
+            copy.wait_recv()
+        yield
+        for copy in (hp_, hm_, gf):
+            copy.wait_recv()
+        yield
+
     def gather_weight(full):
         one, two, both = (0, 48), (48, 32), (0, DPW)
 
@@ -193,6 +235,7 @@
         yield
 
     scale = 1.0 / math.sqrt(16 * PIX)
+    lane20 = lax.broadcasted_iota(jnp.int32, (20, 128), 1)
 
     def scatter_grad(n, grad_out, p):
         c = send(gr.at[n, :, 1 - core], gc.at[n], CN)
@@ -223,9 +266,21 @@
         total = (mine(xh) + gd[n].astype(F32)) * scale
         rest = total[:, 384:512]
         for q in range(3):
-            grad_out[p * 3 + q, :, 0:128] = total[:, q * 128 : q * 128 + 128]
             turned = rest if q == 0 else pltpu.roll(rest, 128 - 32 * q, 1)
-            grad_out[p * 3 + q, :, 128:160] = turned[:, 0:32]
+            flat[0] = total[:, q * 128 : q * 128 + 128]
+            flat[1] = turned
+            main = [flat[0, pl.ds(i, 20, stride=4)] for i in range(4)]
+            tail = [flat[1, pl.ds(i, 20, stride=4)] for i in range(4)]
+            pieces = [main[0]]
+            for i in range(1, 4):
+                shifted = pltpu.roll(main[i], 32 * i, 1)
+                low = pltpu.roll(tail[i - 1], 32 * (i - 1), 1)
+                low = jnp.where(lane20 < 32 * (i - 1), carried, low) if i > 1 else low
+                pieces.append(jnp.where(lane20 < 32 * i, low, shifted))
+                carried = shifted
+            pieces.append(jnp.where(lane20 < 96, carried, pltpu.roll(tail[3], 96, 1)))
+            for j in range(5):
+                grad_out[pl.ds((p * 3 + q) * 100 + j, 20, stride=5)] = pieces[j]
         yield
 
     def step(*work):
@@ -253,7 +308,7 @@
 
     get_img = gather_rows(img, imgf, 0)
     get_w1 = gather_weight(w1)
-    get_cot = gather_rows(cot, cotp, W)
+    get_cot = gather_rows_late(cot, cotp, W)
     get_w2 = gather_weight(w2)
     step(get_w1, get_img, get_img, get_w1, get_w2, get_cot)
 
@@ -305,18 +360,18 @@
     factor = lax.rsqrt(group_mean(total, groups) + EPS)
 
     def img_rows(i):
-        return imgf[pl.ds(pl.multiple_of(i * 16, 16), 16)].astype(F32)
+        return imgf[pl.ds(pl.multiple_of(i * 32, 16), 32)].astype(F32)
 
     def activate_rows(i, carry):
         u = (img_rows(i) - center) * factor
-        actp[pl.ds(pl.multiple_of(W + i * 16, 16), 16)] = (u / (1.0 + jnp.exp(-u))).astype(BF16)
+        actp[pl.ds(pl.multiple_of(W + i * 32, 16), 32)] = (u / (1.0 + jnp.exp(-u))).astype(BF16)
         return carry
 
-    lax.fori_loop(0, PIX // 16, activate_rows, 0)
+    lax.fori_loop(0, PIX // 32, activate_rows, 0)
     step(get_cot, get_cot, get_cot, get_w2, get_w2)
     step(get_w1)
 
-    MT = 288
+    MT = 576
 
     def conv_tiles(source, weight, flip, begin=0, end=PIX // MT):
         def tile(i, carry):
@@ -394,6 +449,7 @@
     coef = dot_nt(hidc[...], bs2[0 : 2 * RANK])
     coef = coef[:, 0:RANK] + coef[:, RANK : 2 * RANK]
     hb[...] = jnp.concatenate([coef[0:HALF], coef[HALF:PIX]], axis=1).astype(BF16)
+    step(get_cot)
     hc0 = send(hb, hx, XN)
 
     def project_act(i, carry):
@@ -405,16 +461,13 @@
         act_t[:, pl.ds(pl.multiple_of(i * AT, 128), AT)] = left.T
         return carry
 
-    project_act(0, 0)
+    lax.fori_loop(0, PIX // AT, project_act, 0)
     hc0.wait_recv()
     hpair[z] = (hb[...].astype(F32) + hx[...].astype(F32)).astype(BF16)
     hcp = send(hpair.at[z], hpair.at[z], ZP)
     hcm = send(hpair.at[z], hpair.at[z], ZM)
-    step(get_cot)
-    project_act(1, 0)
-    project_act(2, 0)
-
-    GT = 640
+
+    GT = 1280
 
     def grad_tiles(n, left_t, buffer, first):
         def tile(i, carry):
@@ -425,7 +478,7 @@
 
         lax.fori_loop(0, C // GT, tile, 0)
 
-    chunks = [scatter_grad(3 + p, g2, p) for p in range(3)] + [scatter_grad(p, g1, p) for p in range(3)]
+    chunks = [scatter_grad(p, g1, p) for p in range(3)] + [scatter_grad(3 + p, g2, p) for p in range(3)]
 
     def move(*which):
         for one in which:
@@ -442,14 +495,57 @@
         return (target.astype(F32) + extra.astype(F32)).astype(BF16)
 
     step(get_w2)
+    step(get_cot, get_cot)
+
+    conv_tiles(cotp, w2, True)
+
+    def grad_rows(h, carry):
+        acc, acc_u = carry
+        main, rest = col_sum(h, from_right, from_left)
+        hg = jnp.concatenate([main, rest], axis=1)
+        u = x[row_at(h)]
+        sig = 1.0 / (1.0 + jnp.exp(-u))
+        d = hg * (sig * (1.0 + u * (1.0 - sig)))
+        du[row_at(h)] = d
+        return acc + fold8(d), acc_u + fold8(d * u)
+
+    acc, acc_u = lax.fori_loop(0, PIX // PART, grad_rows, (zero_acc, zero_acc))
+    mean_d, mean_du = group_mean(acc, groups_x), group_mean(acc_u, groups_x)
+
+    def pre_rows(h, carry):
+        pre = factor_x * (du[row_at(h)] - mean_d - x[row_at(h)] * mean_du)
+        pre = jnp.where(real, pre, 0.0)
+        spread_cols(pp, h, pre[:, 0:128], pre[:, 128:256], from_right, from_left)
+        return carry
+
+    lax.fori_loop(0, PIX // PART, pre_rows, 0)
+
+
+    grad_tiles(0, act_t, pp, 2 * W)
+    move(0)
     conv_second(z2)
     hcp.wait_recv()
     hfp = send(hpair.at[zm, pl.ds(0, 288)], hpair.at[zm, pl.ds(0, 288)], ZP)
     hcm.wait_recv()
     hfm = send(hpair.at[zp, pl.ds(288, 288)], hpair.at[zp, pl.ds(288, 288)], ZM)
     oap, oam = send(o.at[z2, 0], qa.at[0], ZP), send(o.at[z2, 1], qa.at[1], ZM)
-
+    move(0)
+    grad_tiles(1, act_t, pp, W)
+    move(1)
     conv_second(zp)
+    move(1, 0)
+    grad_tiles(2, act_t, pp, 0)
+    move(2)
+    conv_second(zm)
+    move(2)
+    oap.wait_recv()
+    o[zp, 0] = add_into(o[zp, 0], qa[0])
+    obp = send(o.at[zp], qb.at[0], ZP)
+    oam.wait_recv()
+    o[zm, 1] = add_into(o[zm, 1], qa[1])
+    obm = send(o.at[zm], qb.at[1], ZM)
+    move(1)
+
     hfp.wait_recv()
     hfm.wait_recv()
 
@@ -467,8 +563,6 @@
 
     lax.fori_loop(0, HALF // PART, project_hidden, 0)
 
-    step(get_cot, get_cot)
-
     def turn_cot(i, carry):
         cot_t[:, pl.ds(pl.multiple_of(i * 128, 128), 128)] = cotp[
             pl.ds(pl.multiple_of(W + i * 128, 16), 128)
@@ -477,71 +571,28 @@
 
     lax.fori_loop(0, PIX // 128, turn_cot, 0)
 
+    move(2, 0)
     grad_tiles(3, cot_t, pp, 0)
-    move(0)
+    move(3)
+    conv_second(z)
+    move(3, 1)
     grad_tiles(4, cot_t, pp, W)
-    move(1, 0)
+    move(4, 2, 4)
     grad_tiles(5, cot_t, pp, 2 * W)
-    move(2, 1)
-    conv_second(zm)
-    move(2)
-    oap.wait_recv()
-    o[zp, 0] = add_into(o[zp, 0], qa[0])
-    obp = send(o.at[zp], qb.at[0], ZP)
-    oam.wait_recv()
-    o[zm, 1] = add_into(o[zm, 1], qa[1])
-    obm = send(o.at[zm], qb.at[1], ZM)
-    move(0)
-
-    conv_tiles(cotp, w2, True, 0, 2)
-    move(1)
-    conv_tiles(cotp, w2, True, 2, 4)
-    move(2)
-
-    def grad_rows(h, carry):
-        acc, acc_u = carry
-        main, rest = col_sum(h, from_right, from_left)
-        hg = jnp.concatenate([main, rest], axis=1)
-        u = x[row_at(h)]
-        sig = 1.0 / (1.0 + jnp.exp(-u))
-        d = hg * (sig * (1.0 + u * (1.0 - sig)))
-        du[row_at(h)] = d
-        return acc + fold8(d), acc_u + fold8(d * u)
-
-    acc, acc_u = lax.fori_loop(0, PIX // PART, grad_rows, (zero_acc, zero_acc))
-    move(0)
-    mean_d, mean_du = group_mean(acc, groups_x), group_mean(acc_u, groups_x)
-
-    def pre_rows(h, carry):
-        pre = factor_x * (du[row_at(h)] - mean_d - x[row_at(h)] * mean_du)
-        pre = jnp.where(real, pre, 0.0)
-        spread_cols(pp, h, pre[:, 0:128], pre[:, 128:256], from_right, from_left)
-        return carry
-
-    lax.fori_loop(0, PIX // PART, pre_rows, 0)
-
-    move(1)
+    move(5, 3, 5, 4)
 
     def band(xx):
         return o[z, xx].astype(F32) + qb[0, xx].astype(F32) + qb[1, xx].astype(F32)
 
-    grad_tiles(0, act_t, pp, 2 * W)
-    move(3)
-    grad_tiles(1, act_t, pp, W)
-    move(4, 3)
-    grad_tiles(2, act_t, pp, 0)
-    move(5, 4, 2)
-    conv_second(z)
-    move(5, 3)
     obp.wait_recv()
     obm.wait_recv()
     qv[...] = band(1 - xl).astype(BF16)
     odx = send(qv, qd, XN)
-
-    move(4, 5, 0, 1, 2, 3, 4, 5)
+    move(0, 1, 2)
+    move(5, 3, 4)
     odx.wait_recv()
     out[...] = (img[...].astype(F32) + (band(xl) + qd[...].astype(F32))).astype(BF16)
-    move(3, 4, 5)
+    move(5, 3, 4, 5)
     for copy in pending:
         copy.wait_send()
 
@@ -554,8 +605,8 @@
         kernel,
         out_shape=(
             jax.ShapeDtypeStruct((BAND, C), BF16),
-            jax.ShapeDtypeStruct((9, DPW, RW), F32),
-            jax.ShapeDtypeStruct((9, DPW, RW), F32),
+            jax.ShapeDtypeStruct((9 * DPW * RW // 128, 128), F32),
+            jax.ShapeDtypeStruct((9 * DPW * RW // 128, 128), F32),
         ),
         in_specs=[pl.BlockSpec(memory_space=pltpu.VMEM)] * 6,
         out_specs=[pl.BlockSpec(memory_space=pltpu.VMEM)] * 3,
@@ -592,6 +643,7 @@
             vmem((3 * RANK, 256)),
             vmem((8, C), F32),
             vmem((8, C), F32),
+            vmem((2, DPW, 128), F32),
             pltpu.SemaphoreType.DMA((N_SEM,)),
             pltpu.SemaphoreType.DMA((N_SEM,)),
         ],

time: 133 us -> 128 us (0.962)
  Pallas kernels: 121 us -> 118 us
    pallas_call x1, Pallas kernels: 121 us -> 118 us  [body(): pl.pallas_call(kernel, out_shape=(jax.ShapeDtypeStruct((BAND, C), BF16),...]
where the time goes in v3:
time: 128 us
  Pallas kernels  118 us (92%)
  local copies, waits for them, and re-layouts  9.43 us (7%)
    pallas_call x1, Pallas kernels, body(): pl.pallas_call(kernel, out_shape=(jax.ShapeDtypeStruct((BAND, C), BF16),...  118 us

profile of v3, /device:TPU:0, one launch (start us, length us, event | category | flops | bytes accessed | tf_op | source)
XLA Modules:
  0.0 127.8 jit_solution(7557215014884792395)
XLA Ops:
  0.6 0.0 copy-start
  0.6 1.0 copy-done
  1.6 0.1 constant_dynamic-slice_fusion
  1.7 0.6 pad.4.b2
  2.3 0.0 copy-start.2
  2.3 2.3 %reshape.29.w1r = bf16[9,80,160]{2,1,0:T(8,128)(2,1)} reshape(bf16[1,1,9,12800]{3,2,1,0:T(8,128)(2,1)} %param.8) | data formatting | bytes 460800 | tf_op jit(solution)/shard_map/reshape | solution.py:656
  4.6 0.0 copy-done.2
  4.6 1.2 reshape.30.w2r
  5.8 117.7 %shard_map.85 = (bf16[144,1280]{1,0:T(8,128)(2,1)}, f32[900,128]{1,0:T(8,128)}, f32[900,128]{1,0:T(8,128)}) custom-call(bf16[144,1280]{1,0:T(8,128)(2,1)} %bitcast.3, bf16[144,1280]{1,0:T(8,128)(2,1)} %bitcast.4, bf16[9,80,160]{2,1,0:T(8,128)(2,1)} %reshape.29.w1r, bf16[9,80,160]{2,1,0:T(8,128)(2,1)} %reshape.30.w2r, f32[64,1280]{1,0:T(8,128)} %b1.1, ...), custom_call_target="tpu_custom_call" | custom-call | tf_op jit(solution)/shard_map/pallas_call | solution.py:604
  123.5 0.0 copy-start.1
  123.5 2.3 %reshape.34 = f32[1,1,9,12800]{3,1,2,0:T(1,128)} reshape(f32[900,128]{1,0:T(8,128)} %get-tuple-element.7) | data formatting | bytes 921600 | tf_op jit(solution)/shard_map/reshape | solution.py:663
  125.8 0.0 copy-done.1
  125.8 0.0 copy-start.3
  125.8 1.2 reshape.35
  127.0 0.0 copy-done.3
  127.0 0.7 copy.14
Async XLA Ops:
  0.6 1.0 copy-start
  2.3 2.3 %copy-start.2 = (bf16[1,1,9,12800]{3,2,1,0:T(8,128)(2,1)S(1)}, bf16[1,1,9,12800]{3,2,1,0:T(8,128)(2,1)}, u32[]{:S(2)}) copy-start(bf16[1,1,9,12800]{3,2,1,0:T(8,128)(2,1)} %param.9) | copy-start | bytes 691204
  123.5 2.3 %copy-start.1 = (f32[900,128]{1,0:T(8,128)S(1)}, f32[900,128]{1,0:T(8,128)}, u32[]{:S(2)}) copy-start(f32[900,128]{1,0:T(8,128)} %get-tuple-element.8) | copy-start | bytes 1382404
  125.8 1.2 copy-start.3

commit v4 on v3

--- a/solution.py
+++ b/solution.py
@@ -368,7 +368,7 @@
         return carry
 
     lax.fori_loop(0, PIX // 32, activate_rows, 0)
-    step(get_cot, get_cot, get_cot, get_w2, get_w2)
+    step(get_cot, get_cot, get_w2, get_w2)
     step(get_w1)
 
     MT = 576
@@ -389,7 +389,7 @@
         lax.fori_loop(begin, end, tile, 0)
 
     conv_tiles(actp, w1, False)
-    step(get_w2, get_cot, get_w2)
+    step(get_w2, get_cot, get_cot, get_w2)
 
     col = lax.broadcasted_iota(jnp.int32, (PART // W, W, 128), 1).reshape(PART, 128)
     lane = lax.broadcasted_iota(jnp.int32, (PART, 128), 1)
@@ -462,10 +462,6 @@
         return carry
 
     lax.fori_loop(0, PIX // AT, project_act, 0)
-    hc0.wait_recv()
-    hpair[z] = (hb[...].astype(F32) + hx[...].astype(F32)).astype(BF16)
-    hcp = send(hpair.at[z], hpair.at[z], ZP)
-    hcm = send(hpair.at[z], hpair.at[z], ZM)
 
     GT = 1280
 
@@ -498,6 +494,10 @@
     step(get_cot, get_cot)
 
     conv_tiles(cotp, w2, True)
+    hc0.wait_recv()
+    hpair[z] = (hb[...].astype(F32) + hx[...].astype(F32)).astype(BF16)
+    hcp = send(hpair.at[z], hpair.at[z], ZP)
+    hcm = send(hpair.at[z], hpair.at[z], ZM)
 
     def grad_rows(h, carry):
         acc, acc_u = carry
@@ -577,9 +577,9 @@
     conv_second(z)
     move(3, 1)
     grad_tiles(4, cot_t, pp, W)
-    move(4, 2, 4)
+    move(4, 2, 4, 3)
     grad_tiles(5, cot_t, pp, 2 * W)
-    move(5, 3, 5, 4)
+    move(5, 0, 1, 5, 4)
 
     def band(xx):
         return o[z, xx].astype(F32) + qb[0, xx].astype(F32) + qb[1, xx].astype(F32)
@@ -588,8 +588,7 @@
     obm.wait_recv()
     qv[...] = band(1 - xl).astype(BF16)
     odx = send(qv, qd, XN)
-    move(0, 1, 2)
-    move(5, 3, 4)
+    move(2, 3, 5, 4)
     odx.wait_recv()
     out[...] = (img[...].astype(F32) + (band(xl) + qd[...].astype(F32))).astype(BF16)
     move(5, 3, 4, 5)

time: 128 us -> 126 us (0.984)
  Pallas kernels: 118 us -> 116 us
    pallas_call x1, Pallas kernels: 118 us -> 116 us  [body(): pl.pallas_call(kernel, out_shape=(jax.ShapeDtypeStruct((BAND, C), BF16),...]
where the time goes in v4:
time: 126 us
  Pallas kernels  116 us (92%)
  local copies, waits for them, and re-layouts  9.43 us (7%)
    pallas_call x1, Pallas kernels, body(): pl.pallas_call(kernel, out_shape=(jax.ShapeDtypeStruct((BAND, C), BF16),...  116 us

profile of v4, /device:TPU:0, one launch (start us, length us, event | category | flops | bytes accessed | tf_op | source)
XLA Modules:
  0.0 126.0 jit_solution(8895844423307967902)
XLA Ops:
  0.6 0.0 copy-start
  0.6 1.0 copy-done
  1.6 0.1 constant_dynamic-slice_fusion
  1.7 0.6 pad.4.b2
  2.3 0.0 copy-start.2
  2.3 2.3 %reshape.29.w1r = bf16[9,80,160]{2,1,0:T(8,128)(2,1)} reshape(bf16[1,1,9,12800]{3,2,1,0:T(8,128)(2,1)} %param.8) | data formatting | bytes 460800 | tf_op jit(solution)/shard_map/reshape | solution.py:655
  4.6 0.0 copy-done.2
  4.6 1.2 reshape.30.w2r
  5.8 115.9 %shard_map.85 = (bf16[144,1280]{1,0:T(8,128)(2,1)}, f32[900,128]{1,0:T(8,128)}, f32[900,128]{1,0:T(8,128)}) custom-call(bf16[144,1280]{1,0:T(8,128)(2,1)} %bitcast.3, bf16[144,1280]{1,0:T(8,128)(2,1)} %bitcast.4, bf16[9,80,160]{2,1,0:T(8,128)(2,1)} %reshape.29.w1r, bf16[9,80,160]{2,1,0:T(8,128)(2,1)} %reshape.30.w2r, f32[64,1280]{1,0:T(8,128)} %b1.1, ...), custom_call_target="tpu_custom_call" | custom-call | tf_op jit(solution)/shard_map/pallas_call | solution.py:603
  121.8 0.0 copy-start.1
  121.8 2.3 %reshape.34 = f32[1,1,9,12800]{3,1,2,0:T(1,128)} reshape(f32[900,128]{1,0:T(8,128)} %get-tuple-element.7) | data formatting | bytes 921600 | tf_op jit(solution)/shard_map/reshape | solution.py:662
  124.1 0.0 copy-done.1
  124.1 0.0 copy-start.3
  124.1 1.2 reshape.35
  125.3 0.0 copy-done.3
  125.3 0.7 copy.14
Async XLA Ops:
  0.6 1.0 copy-start
  2.3 2.3 %copy-start.2 = (bf16[1,1,9,12800]{3,2,1,0:T(8,128)(2,1)S(1)}, bf16[1,1,9,12800]{3,2,1,0:T(8,128)(2,1)}, u32[]{:S(2)}) copy-start(bf16[1,1,9,12800]{3,2,1,0:T(8,128)(2,1)} %param.9) | copy-start | bytes 691204
  121.8 2.3 %copy-start.1 = (f32[900,128]{1,0:T(8,128)S(1)}, f32[900,128]{1,0:T(8,128)}, u32[]{:S(2)}) copy-start(f32[900,128]{1,0:T(8,128)} %get-tuple-element.8) | copy-start | bytes 1382404
  124.1 1.2 copy-start.3

commit v5 on v4

--- a/solution.py
+++ b/solution.py
@@ -449,7 +449,6 @@
     coef = dot_nt(hidc[...], bs2[0 : 2 * RANK])
     coef = coef[:, 0:RANK] + coef[:, RANK : 2 * RANK]
     hb[...] = jnp.concatenate([coef[0:HALF], coef[HALF:PIX]], axis=1).astype(BF16)
-    step(get_cot)
     hc0 = send(hb, hx, XN)
 
     def project_act(i, carry):
@@ -461,7 +460,9 @@
         act_t[:, pl.ds(pl.multiple_of(i * AT, 128), AT)] = left.T
         return carry
 
-    lax.fori_loop(0, PIX // AT, project_act, 0)
+    project_act(0, 0)
+    step(get_cot)
+    lax.fori_loop(1, PIX // AT, project_act, 0)
 
     GT = 1280
 
@@ -571,15 +572,15 @@
 
     lax.fori_loop(0, PIX // 128, turn_cot, 0)
 
-    move(2, 0)
+    move(0)
     grad_tiles(3, cot_t, pp, 0)
-    move(3)
+    move(3, 2)
     conv_second(z)
     move(3, 1)
     grad_tiles(4, cot_t, pp, W)
-    move(4, 2, 4, 3)
+    move(4, 0, 4, 3, 2)
     grad_tiles(5, cot_t, pp, 2 * W)
-    move(5, 0, 1, 5, 4)
+    move(5, 1, 5, 4)
 
     def band(xx):
         return o[z, xx].astype(F32) + qb[0, xx].astype(F32) + qb[1, xx].astype(F32)
@@ -588,10 +589,10 @@
     obm.wait_recv()
     qv[...] = band(1 - xl).astype(BF16)
     odx = send(qv, qd, XN)
-    move(2, 3, 5, 4)
+    move(2, 3, 5, 4, 5)
     odx.wait_recv()
     out[...] = (img[...].astype(F32) + (band(xl) + qd[...].astype(F32))).astype(BF16)
-    move(5, 3, 4, 5)
+    move(3, 4, 5)
     for copy in pending:
         copy.wait_send()
 

time: 126 us -> 126 us (level)
  no operation moved by 1% of the time
where the time goes in v5:
time: 126 us; the launch traced here: 125 us
  Pallas kernels  115 us (91%)
  local copies, waits for them, and re-layouts  9.43 us (7%)
    pallas_call x1, Pallas kernels, body(): pl.pallas_call(kernel, out_shape=(jax.ShapeDtypeStruct((BAND, C), BF16),...  115 us

profile of v5, /device:TPU:0, one launch (start us, length us, event | category | flops | bytes accessed | tf_op | source)
XLA Modules:
  0.0 125.0 jit_solution(2002992325054933743)
XLA Ops:
  0.6 0.0 copy-start
  0.6 1.0 copy-done
  1.6 0.1 constant_dynamic-slice_fusion
  1.7 0.6 pad.4.b2
  2.3 0.0 copy-start.2
  2.3 2.3 %reshape.29.w1r = bf16[9,80,160]{2,1,0:T(8,128)(2,1)} reshape(bf16[1,1,9,12800]{3,2,1,0:T(8,128)(2,1)} %param.8) | data formatting | bytes 460800 | tf_op jit(solution)/shard_map/reshape | solution.py:656
  4.6 0.0 copy-done.2
  4.6 1.2 reshape.30.w2r
  5.8 114.9 %shard_map.85 = (bf16[144,1280]{1,0:T(8,128)(2,1)}, f32[900,128]{1,0:T(8,128)}, f32[900,128]{1,0:T(8,128)}) custom-call(bf16[144,1280]{1,0:T(8,128)(2,1)} %bitcast.3, bf16[144,1280]{1,0:T(8,128)(2,1)} %bitcast.4, bf16[9,80,160]{2,1,0:T(8,128)(2,1)} %reshape.29.w1r, bf16[9,80,160]{2,1,0:T(8,128)(2,1)} %reshape.30.w2r, f32[64,1280]{1,0:T(8,128)} %b1.1, ...), custom_call_target="tpu_custom_call" | custom-call | tf_op jit(solution)/shard_map/pallas_call | solution.py:604
  120.8 0.0 copy-start.1
  120.8 2.3 %reshape.34 = f32[1,1,9,12800]{3,1,2,0:T(1,128)} reshape(f32[900,128]{1,0:T(8,128)} %get-tuple-element.7) | data formatting | bytes 921600 | tf_op jit(solution)/shard_map/reshape | solution.py:663
  123.1 0.0 copy-done.1
  123.1 0.0 copy-start.3
  123.1 1.2 reshape.35
  124.3 0.0 copy-done.3
  124.3 0.7 copy.14
Async XLA Ops:
  0.6 1.0 copy-start
  2.3 2.3 %copy-start.2 = (bf16[1,1,9,12800]{3,2,1,0:T(8,128)(2,1)S(1)}, bf16[1,1,9,12800]{3,2,1,0:T(8,128)(2,1)}, u32[]{:S(2)}) copy-start(bf16[1,1,9,12800]{3,2,1,0:T(8,128)(2,1)} %param.9) | copy-start | bytes 691204
  120.8 2.3 %copy-start.1 = (f32[900,128]{1,0:T(8,128)S(1)}, f32[900,128]{1,0:T(8,128)}, u32[]{:S(2)}) copy-start(f32[900,128]{1,0:T(8,128)} %get-tuple-element.8) | copy-start | bytes 1382404
  123.1 1.2 copy-start.3
